TPU v7x, 1024 devices: a whole 4x4x32 slice. The times are simulated.
1024 devices in a mesh: curve: 256 (over x, z, core), group: 4 (over y).
Axes of the slice: x: 4, y: 4, z: 32, core: 2. Of those that a mesh axis runs over, the one named last changes fastest.
Arguments:
- field: float32 [3, 4096, 128, 128], P(None, 'curve', 'group'), may hold values from -6 to 6
- source: float32 [3, 4096, 128, 128], P(None, 'curve', 'group'), may hold values from -16 to 16
- mass: float32 [4096, 128, 128], P('curve', 'group'), may hold values from 0.5 to 8
- interp: float32 [4, 128, 128], replicated, may hold values from -0.5 to 1.5
- parent_list: int32 [256, 4, 4, 16], P('curve', 'group'), may hold values from 0 to 511
- child_list: int32 [256, 4, 4, 16], P('curve', 'group'), may hold values from 0 to 511
- child_kind: int32 [256, 4, 4, 16], P('curve', 'group'), may hold values from 0 to 3
- counts: int32 [256, 4, 4], P('curve', 'group'), may hold values from 0 to 16, as said below
Outputs:
- cycle: float32 [3, 4096, 128, 128], P(None, 'curve', 'group')
Inputs may be any that keep to these rules, and one draw needn't show every extreme that they name: `parent_list`: local block index x * 32 + y on the device that owns the parent. `child_list`: local block index x * 32 + y on the device that owns the child. `counts`: in every draw, in each curve segment one destination group receives 16 live slots from every source group; every other destination group receives at most 8 live slots from each source group.
All inputs are finite; a program needn't handle non-finite values.
Results may differ from a plain program's by a relative error of at most 0.0001.
Values sent between devices are 32-bit elements; how exact they have to be, the bound alone decides.
No kernel may reach another device: no remote copies, remote signals or barrier semaphores. Data moves between devices by JAX's collectives and lax.ppermute only.
A program may use at most 32 MiB of HBM per device.

v0:
```python
import jax
import jax.numpy as jnp
from jax import lax
from jax.sharding import PartitionSpec as P

SWEEPS = 2


OMEGA = 2.0 / 3.0


def extended(array, sides, width):
    edges = {}
    for axis, dim in sides:
        count, length = (lax.axis_size(axis), array.shape[dim])
        up = [(i, (i + 1) % count) for i in range(count - 1)]
        last = lax.slice_in_dim(array, length - width, length, axis=dim)
        leading = lax.slice_in_dim(array, 0, width, axis=dim)
        edges[dim] = (
            lax.ppermute(last, axis, up),
            lax.ppermute(leading, axis, [(b, a) for a, b in up]),
        )
    done = []
    for _, dim in sides:
        low, high = edges[dim]
        around = [(width, width) if d in done else (0, 0) for d in range(array.ndim)]
        array = jnp.concatenate([jnp.pad(low, around), array, jnp.pad(high, around)], axis=dim)
        done.append(dim)
    return array


def relax(padded, source, mass):
    centre = padded[:, 1:-1, 1:-1, :]
    beside = (
        padded[:, 2:, 1:-1, :]
        + padded[:, :-2, 1:-1, :]
        + padded[:, 1:-1, 2:, :]
        + padded[:, 1:-1, :-2, :]
    )
    z_pair = jnp.pad(centre, ((0, 0), (0, 0), (0, 0), (1, 1)))
    beside = beside + z_pair[..., 2:] + z_pair[..., :-2]
    diag_total = 6.0 + mass
    applied = diag_total * centre - beside
    return centre + OMEGA * (source - applied) / diag_total


def stacked(interp, order):
    kind_total = interp.shape[0]
    node_count = interp.shape[1]
    return jnp.transpose(interp, order).reshape(node_count, kind_total * node_count)


def pick_kind(product, onehot):
    return jnp.sum(product * onehot[None, :, :, :, None], axis=3)


def local(field, source, mass, interp, parent_list, child_list, child_kind, counts):
    components, rows_x, rows_y, node_count = field.shape
    groups = lax.axis_size("group")
    slot_count = parent_list.shape[3]
    kind_total = interp.shape[0]
    blocks = field.reshape(components, rows_x * rows_y, node_count)
    active = (jnp.arange(slot_count, dtype=jnp.int32)[None, :] < counts.reshape(groups, 1)).astype(
        jnp.float32
    )
    onehot = (
        child_kind.reshape(groups, slot_count, 1)
        == jnp.arange(kind_total, dtype=jnp.int32)[None, None, :]
    ).astype(jnp.float32)
    child_index = child_list.reshape(groups * slot_count)
    parent_index = parent_list.reshape(groups * slot_count)
    picked = (
        jnp.take(blocks, parent_index, axis=1).reshape(components, groups, slot_count, node_count)
        * active[None, :, :, None]
    )
    forward_table = stacked(interp, (1, 0, 2))
    arrived = lax.all_to_all(picked, "group", split_axis=1, concat_axis=1, tiled=True)
    shape = arrived.shape
    product = jnp.dot(
        arrived.reshape(-1, shape[3]),
        forward_table,
        precision=lax.Precision.HIGHEST,
        preferred_element_type=jnp.float32,
    )
    products = product.reshape(shape[0], shape[1], shape[2], kind_total, shape[3])
    hanging = pick_kind(products, onehot).reshape(components, groups * slot_count, node_count)
    constrained = (
        blocks.at[:, child_index].add(hanging).reshape(components, rows_x, rows_y, node_count)
    )
    state = constrained
    for sweep_index in range(SWEEPS):
        padded = extended(state, (("curve", 1), ("group", 2)), 1)
        state = relax(padded, source, mass)
    correction = (state - constrained).reshape(components, rows_x * rows_y, node_count)
    back_table = stacked(interp, (2, 0, 1))
    chosen = jnp.take(correction, child_index, axis=1)
    product = jnp.dot(
        chosen.reshape(-1, node_count),
        back_table,
        precision=lax.Precision.HIGHEST,
        preferred_element_type=jnp.float32,
    )
    restricted = pick_kind(
        product.reshape(components, groups, slot_count, kind_total, node_count), onehot
    )
    arrived = lax.all_to_all(restricted, "group", split_axis=1, concat_axis=1, tiled=True)
    arrived = arrived * active[None, :, :, None]
    summed = (
        jnp.zeros_like(blocks)
        .at[:, parent_index]
        .add(arrived.reshape(components, groups * slot_count, node_count))
    )
    return state + summed.reshape(components, rows_x, rows_y, node_count)


def solution(mesh):
    in_specs = (
        P(None, "curve", "group", None),
        P(None, "curve", "group", None),
        P("curve", "group", None),
        P(),
        P("curve", "group", None, None),
        P("curve", "group", None, None),
        P("curve", "group", None, None),
        P("curve", "group", None),
    )
    out_specs = P(None, "curve", "group", None)
    return jax.shard_map(local, mesh=mesh, in_specs=in_specs, out_specs=out_specs, check_vma=False)
```

profile of v0, /device:TPU:6, one launch (start us, length us, event | category | flops | bytes accessed | tf_op | source)
XLA Modules:
  0.0 78.2 jit_solution(415705459906261046)
XLA Ops:
  0.0 0.8 reshape.143
  0.8 0.8 reshape.150
  1.6 1.7 %copy.83 = f32[3,16,32,128]{3,0,2,1:T(4,128)S(1)} copy(f32[3,16,32,128]{3,2,1,0:T(8,128)} %param.10) | data formatting | bytes 1572864 | tf_op args[0]
  3.4 0.7 gather_fusion
  4.9 4.5 %all-to-all-start = ((f32[3,4,16,128]{3,2,0,1:T(8,128)}), f32[3,4,16,128]{3,2,0,1:T(8,128)S(1)}, u32[]{:S(2)}, u32[]{:S(2)}) async-start(f32[3,4,16,128]{3,2,0,1:T(8,128)} %copy.85), calls=%async_computation | async-start | bytes 196608 | tf_op jit(solution)/shard_map/all_to_all | solution.py:77
  9.7 5.5 %all-to-all-done = f32[3,4,16,128]{3,2,0,1:T(8,128)S(1)} async-done(((f32[3,4,16,128]{3,2,0,1:T(8,128)}), f32[3,4,16,128]{3,2,0,1:T(8,128)S(1)}, u32[]{:S(2)}, u32[]{:S(2)}) %all-to-all-start) | async-done | bytes 98336 | tf_op jit(solution)/shard_map/all_to_all | solution.py:77
  15.8 2.7 %scatter_fusion = f32[3,512,128]{2,0,1:T(4,128)S(1)} fusion(f32[3,512,128]{2,0,1:T(4,128)S(1)} %bitcast.55, s32[64]{0:T(128)S(1)} %fusion.30, f32[64,3,128]{2,1,0:T(4,128)S(1)} %bitcast.63), kind=kCustom, calls=%fused_computation.2 | custom fusion | flops 24576 | bytes 295168 | tf_op jit(solution)/shard_map/scatter-add | solution.py:88
  18.6 2.1 %collective-permute-start.1 = (f32[3,1,32,128]{3,2,1,0:T(8,128)S(1)}, f32[3,1,32,128]{3,2,1,0:T(8,128)S(1)}, u32[]{:S(2)}, u32[]{:S(2)}) collective-permute-start(f32[3,1,32,128]{3,2,1,0:T(8,128)S(1)} %get-tuple-element.15), channel_id=1, source_target_pairs={{0,4},{4,8},{8,12},{12,16},{16,20},{20,24},{24,28},{28,32},{32,36}... | collective-permute-start | bytes 147464 | tf_op jit(solution)/shard_map/ppermute | solution.py:20
  20.7 17.0 %collective-permute-start = (f32[3,1,32,128]{3,2,1,0:T(8,128)S(1)}, f32[3,1,32,128]{3,2,1,0:T(8,128)S(1)}, u32[]{:S(2)}, u32[]{:S(2)}) collective-permute-start(f32[3,1,32,128]{3,2,1,0:T(8,128)S(1)} %get-tuple-element.14), channel_id=1, source_target_pairs={{4,0},{8,4},{12,8},{16,12},{20,16},{24,20},{28,24},{32,28},{36,32}... | collective-permute-start | bytes 147464 | tf_op jit(solution)/shard_map/ppermute | solution.py:21
  37.7 1.3 %collective-permute-start.2 = (f32[3,16,1,128]{3,2,1,0:T(1,128)S(1)}, f32[3,16,1,128]{3,2,1,0:T(1,128)S(1)}, u32[]{:S(2)}, u32[]{:S(2)}) collective-permute-start(f32[3,16,1,128]{3,2,1,0:T(1,128)S(1)} %get-tuple-element.12), channel_id=1, source_target_pairs={{1,0},{2,1},{3,2},{5,4},{6,5},{7,6},{9,8},{10,9},{11,10},{13,12},{... | collective-permute-start | bytes 73736 | tf_op jit(solution)/shard_map/ppermute | solution.py:21
  39.0 4.5 %collective-permute-start.3 = (f32[3,16,1,128]{3,2,1,0:T(1,128)S(1)}, f32[3,16,1,128]{3,2,1,0:T(1,128)S(1)}, u32[]{:S(2)}, u32[]{:S(2)}) collective-permute-start(f32[3,16,1,128]{3,2,1,0:T(1,128)S(1)} %get-tuple-element.13), channel_id=1, source_target_pairs={{0,1},{1,2},{2,3},{4,5},{5,6},{6,7},{8,9},{9,10},{10,11},{12,13},{... | collective-permute-start | bytes 73736 | tf_op jit(solution)/shard_map/ppermute | solution.py:20
  43.7 1.3 %collective-permute-done.3 = f32[3,16,1,128]{3,2,1,0:T(1,128)S(1)} collective-permute-done((f32[3,16,1,128]{3,2,1,0:T(1,128)S(1)}, f32[3,16,1,128]{3,2,1,0:T(1,128)S(1)}, u32[]{:S(2)}, u32[]{:S(2)}) %collective-permute-start.3) | collective-permute-done | bytes 24608 | tf_op jit(solution)/shard_map/ppermute | solution.py:20
  45.1 0.7 fusion.8
  45.8 2.9 %collective-permute-start.4 = (f32[3,1,32,128]{3,2,1,0:T(8,128)S(1)}, f32[3,1,32,128]{3,2,1,0:T(8,128)S(1)}, u32[]{:S(2)}, u32[]{:S(2)}) collective-permute-start(f32[3,1,32,128]{3,2,1,0:T(8,128)S(1)} %get-tuple-element.11), channel_id=1, source_target_pairs={{4,0},{8,4},{12,8},{16,12},{20,16},{24,20},{28,24},{32,28},{36,32}... | collective-permute-start | bytes 147464 | tf_op jit(solution)/shard_map/ppermute | solution.py:21
  48.7 1.9 %collective-permute-start.5 = (f32[3,1,32,128]{3,2,1,0:T(8,128)S(1)}, f32[3,1,32,128]{3,2,1,0:T(8,128)S(1)}, u32[]{:S(2)}, u32[]{:S(2)}) collective-permute-start(f32[3,1,32,128]{3,2,1,0:T(8,128)S(1)} %get-tuple-element.10), channel_id=1, source_target_pairs={{0,4},{4,8},{8,12},{12,16},{16,20},{20,24},{24,28},{28,32},{32,36}... | collective-permute-start | bytes 147464 | tf_op jit(solution)/shard_map/ppermute | solution.py:20
  50.7 1.3 %collective-permute-start.6 = (f32[3,16,1,128]{3,2,1,0:T(1,128)S(1)}, f32[3,16,1,128]{3,2,1,0:T(1,128)S(1)}, u32[]{:S(2)}, u32[]{:S(2)}) collective-permute-start(f32[3,16,1,128]{3,2,1,0:T(1,128)S(1)} %get-tuple-element.8), channel_id=1, source_target_pairs={{1,0},{2,1},{3,2},{5,4},{6,5},{7,6},{9,8},{10,9},{11,10},{13,12},{... | collective-permute-start | bytes 73736 | tf_op jit(solution)/shard_map/ppermute | solution.py:21
  52.0 4.5 %collective-permute-start.7 = (f32[3,16,1,128]{3,2,1,0:T(1,128)S(1)}, f32[3,16,1,128]{3,2,1,0:T(1,128)S(1)}, u32[]{:S(2)}, u32[]{:S(2)}) collective-permute-start(f32[3,16,1,128]{3,2,1,0:T(1,128)S(1)} %get-tuple-element.9), channel_id=1, source_target_pairs={{0,1},{1,2},{2,3},{4,5},{5,6},{6,7},{8,9},{9,10},{10,11},{12,13},{... | collective-permute-start | bytes 73736 | tf_op jit(solution)/shard_map/ppermute | solution.py:20
  56.6 1.4 %collective-permute-done.7 = f32[3,16,1,128]{3,2,1,0:T(1,128)S(1)} collective-permute-done((f32[3,16,1,128]{3,2,1,0:T(1,128)S(1)}, f32[3,16,1,128]{3,2,1,0:T(1,128)S(1)}, u32[]{:S(2)}, u32[]{:S(2)}) %collective-permute-start.7) | collective-permute-done | bytes 24608 | tf_op jit(solution)/shard_map/ppermute | solution.py:20
  58.6 1.6 %fusion.32 = (f32[3,16,32,128]{3,2,1,0:T(8,128)S(1)}, f32[3,16,32,128]{3,2,1,0:T(8,128)S(1)}) fusion(f32[3,16,32,128]{3,2,1,0:T(8,128)S(1)} %fusion.8, f32[3,16,32,128]{3,2,1,0:T(8,128)S(1)} %copy-done, f32[3,1,32,128]{3,2,1,0:T(8,128)S(1)} %collective-permute-done.4, f32[3,1,32,128]{3,2,1,0:T(8,128)S(1)} %collective-permute-done.5, ...), kind=kLoop, calls=%fused_computation.78 | loop fusion | flops 5111808 | bytes 4341760 | tf_op jit(solution)/shard_map/sub | solution.py:94
  60.8 0.7 gather_fusion.1
  62.7 5.6 %all-to-all-start.1 = ((f32[3,4,16,128]{3,2,0,1:T(8,128)}), f32[3,4,16,128]{3,2,0,1:T(8,128)S(1)}, u32[]{:S(2)}, u32[]{:S(2)}) async-start(f32[3,4,16,128]{3,2,0,1:T(8,128)} %copy.102), calls=%async_computation.1 | async-start | bytes 196608 | tf_op jit(solution)/shard_map/all_to_all | solution.py:106
  68.4 5.8 %all-to-all-done.1 = f32[3,4,16,128]{3,2,0,1:T(8,128)S(1)} async-done(((f32[3,4,16,128]{3,2,0,1:T(8,128)}), f32[3,4,16,128]{3,2,0,1:T(8,128)S(1)}, u32[]{:S(2)}, u32[]{:S(2)}) %all-to-all-start.1) | async-done | bytes 98336 | tf_op jit(solution)/shard_map/all_to_all | solution.py:106
  74.5 2.7 %scatter_fusion.1 = f32[3,512,128]{2,0,1:T(4,128)S(1)} fusion(f32[3,512,128]{2,0,1:T(4,128)S(1)} %broadcast_in_dim.11, s32[64]{0:T(128)S(1)} %fusion.31, f32[64,3,128]{2,1,0:T(4,128)S(1)} %copy.104), kind=kCustom, calls=%fused_computation.3 | custom fusion | flops 24576 | bytes 295168 | tf_op jit(solution)/shard_map/scatter-add | solution.py:111
  77.2 1.0 %copy_add_fusion = f32[3,16,32,128]{3,2,1,0:T(8,128)} fusion(f32[3,16,32,128]{3,2,1,0:T(8,128)S(1)} %get-tuple-element.7, f32[3,16,32,128]{3,0,2,1:T(4,128)S(1)} %bitcast.59), kind=kLoop, calls=%fused_computation.50 | loop fusion | flops 196608 | bytes 2359296 | tf_op jit(solution)/shard_map/add | solution.py:113
  (59 shorter events, 4.9 us)
Async XLA Ops:
  0.0 3.3 %copy-start.9 = (s32[1,1,4]{2,1,0:T(1,128)S(1)}, s32[1,1,4]{2,1,0:T(1,128)}, u32[]{:S(2)}) copy-start(s32[1,1,4]{2,1,0:T(1,128)} %param.17) | copy-start | bytes 52
  1.6 7.8 %copy-start.6 = (s32[1,1,4,16]{3,2,1,0:T(4,128)S(1)}, s32[1,1,4,16]{3,2,1,0:T(4,128)}, u32[]{:S(2)}) copy-start(s32[1,1,4,16]{3,2,1,0:T(4,128)} %param.15) | copy-start | bytes 772
  1.6 7.9 %copy-start.8 = (s32[1,1,4,16]{3,2,1,0:T(4,128)S(1)}, s32[1,1,4,16]{3,2,1,0:T(4,128)}, u32[]{:S(2)}) copy-start(s32[1,1,4,16]{3,2,1,0:T(4,128)} %param.16) | copy-start | bytes 772
  1.6 7.9 %copy-start.4 = (f32[16,32,128]{2,1,0:T(8,128)S(1)}, f32[16,32,128]{2,1,0:T(8,128)}, u32[]{:S(2)}) copy-start(f32[16,32,128]{2,1,0:T(8,128)} %param.12) | copy-start | bytes 786436
  3.3 6.2 %copy-start.2 = (f32[4,128,128]{2,1,0:T(8,128)S(1)}, f32[4,128,128]{2,1,0:T(8,128)}, u32[]{:S(2)}) copy-start(f32[4,128,128]{2,1,0:T(8,128)} %param.13) | copy-start | bytes 786436
  4.9 10.3 %all-to-all-start = ((f32[3,4,16,128]{3,2,0,1:T(8,128)}), f32[3,4,16,128]{3,2,0,1:T(8,128)S(1)}, u32[]{:S(2)}, u32[]{:S(2)}) async-start(f32[3,4,16,128]{3,2,0,1:T(8,128)} %copy.85), calls=%async_computation | async-start | bytes 196608 | tf_op jit(solution)/shard_map/all_to_all | solution.py:77
  9.5 35.5 %copy-start.1 = (f32[16,32,128]{2,1,0:T(8,128)}, f32[16,32,128]{2,1,0:T(8,128)S(1)}, u32[]{:S(2)}) copy-start(f32[16,32,128]{2,1,0:T(8,128)S(1)} %broadcast_add_fusion) | copy-start | bytes 786436
  18.6 26.4 %copy-start = (f32[3,16,32,128]{3,2,1,0:T(8,128)S(1)}, f32[3,16,32,128]{3,2,1,0:T(8,128)}, u32[]{:S(2)}) copy-start(f32[3,16,32,128]{3,2,1,0:T(8,128)} %param.11) | copy-start | bytes 2359300
  18.6 24.9 %collective-permute-start.1 = (f32[3,1,32,128]{3,2,1,0:T(8,128)S(1)}, f32[3,1,32,128]{3,2,1,0:T(8,128)S(1)}, u32[]{:S(2)}, u32[]{:S(2)}) collective-permute-start(f32[3,1,32,128]{3,2,1,0:T(8,128)S(1)} %get-tuple-element.15), channel_id=1, source_target_pairs={{0,4},{4,8},{8,12},{12,16},{16,20},{20,24},{24,28},{28,32},{32,36}... | collective-permute-start | bytes 147464 | tf_op jit(solution)/shard_map/ppermute | solution.py:20
  20.7 23.0 %collective-permute-start = (f32[3,1,32,128]{3,2,1,0:T(8,128)S(1)}, f32[3,1,32,128]{3,2,1,0:T(8,128)S(1)}, u32[]{:S(2)}, u32[]{:S(2)}) collective-permute-start(f32[3,1,32,128]{3,2,1,0:T(8,128)S(1)} %get-tuple-element.14), channel_id=1, source_target_pairs={{4,0},{8,4},{12,8},{16,12},{20,16},{24,20},{28,24},{32,28},{36,32}... | collective-permute-start | bytes 147464 | tf_op jit(solution)/shard_map/ppermute | solution.py:21
  37.7 6.0 %collective-permute-start.2 = (f32[3,16,1,128]{3,2,1,0:T(1,128)S(1)}, f32[3,16,1,128]{3,2,1,0:T(1,128)S(1)}, u32[]{:S(2)}, u32[]{:S(2)}) collective-permute-start(f32[3,16,1,128]{3,2,1,0:T(1,128)S(1)} %get-tuple-element.12), channel_id=1, source_target_pairs={{1,0},{2,1},{3,2},{5,4},{6,5},{7,6},{9,8},{10,9},{11,10},{13,12},{... | collective-permute-start | bytes 73736 | tf_op jit(solution)/shard_map/ppermute | solution.py:21
  39.0 6.1 %collective-permute-start.3 = (f32[3,16,1,128]{3,2,1,0:T(1,128)S(1)}, f32[3,16,1,128]{3,2,1,0:T(1,128)S(1)}, u32[]{:S(2)}, u32[]{:S(2)}) collective-permute-start(f32[3,16,1,128]{3,2,1,0:T(1,128)S(1)} %get-tuple-element.13), channel_id=1, source_target_pairs={{0,1},{1,2},{2,3},{4,5},{5,6},{6,7},{8,9},{9,10},{10,11},{12,13},{... | collective-permute-start | bytes 73736 | tf_op jit(solution)/shard_map/ppermute | solution.py:20
  43.7 12.8 %copy-start.7 = (s32[1,1,4,16]{3,2,1,0:T(4,128)S(1)}, s32[1,1,4,16]{3,2,1,0:T(4,128)}, u32[]{:S(2)}) copy-start(s32[1,1,4,16]{3,2,1,0:T(4,128)} %param.14) | copy-start | bytes 772
  45.8 12.2 %collective-permute-start.4 = (f32[3,1,32,128]{3,2,1,0:T(8,128)S(1)}, f32[3,1,32,128]{3,2,1,0:T(8,128)S(1)}, u32[]{:S(2)}, u32[]{:S(2)}) collective-permute-start(f32[3,1,32,128]{3,2,1,0:T(8,128)S(1)} %get-tuple-element.11), channel_id=1, source_target_pairs={{4,0},{8,4},{12,8},{16,12},{20,16},{24,20},{28,24},{32,28},{36,32}... | collective-permute-start | bytes 147464 | tf_op jit(solution)/shard_map/ppermute | solution.py:21
  48.7 9.9 %collective-permute-start.5 = (f32[3,1,32,128]{3,2,1,0:T(8,128)S(1)}, f32[3,1,32,128]{3,2,1,0:T(8,128)S(1)}, u32[]{:S(2)}, u32[]{:S(2)}) collective-permute-start(f32[3,1,32,128]{3,2,1,0:T(8,128)S(1)} %get-tuple-element.10), channel_id=1, source_target_pairs={{0,4},{4,8},{8,12},{12,16},{16,20},{20,24},{24,28},{28,32},{32,36}... | collective-permute-start | bytes 147464 | tf_op jit(solution)/shard_map/ppermute | solution.py:20
  50.7 6.0 %collective-permute-start.6 = (f32[3,16,1,128]{3,2,1,0:T(1,128)S(1)}, f32[3,16,1,128]{3,2,1,0:T(1,128)S(1)}, u32[]{:S(2)}, u32[]{:S(2)}) collective-permute-start(f32[3,16,1,128]{3,2,1,0:T(1,128)S(1)} %get-tuple-element.8), channel_id=1, source_target_pairs={{1,0},{2,1},{3,2},{5,4},{6,5},{7,6},{9,8},{10,9},{11,10},{13,12},{... | collective-permute-start | bytes 73736 | tf_op jit(solution)/shard_map/ppermute | solution.py:21
  52.0 6.1 %collective-permute-start.7 = (f32[3,16,1,128]{3,2,1,0:T(1,128)S(1)}, f32[3,16,1,128]{3,2,1,0:T(1,128)S(1)}, u32[]{:S(2)}, u32[]{:S(2)}) collective-permute-start(f32[3,16,1,128]{3,2,1,0:T(1,128)S(1)} %get-tuple-element.9), channel_id=1, source_target_pairs={{0,1},{1,2},{2,3},{4,5},{5,6},{6,7},{8,9},{9,10},{10,11},{12,13},{... | collective-permute-start | bytes 73736 | tf_op jit(solution)/shard_map/ppermute | solution.py:20
  58.0 0.6 copy-start.5
  60.2 1.4 %copy-start.3 = (f32[4,128,128]{2,1,0:T(8,128)S(1)}, f32[4,128,128]{2,1,0:T(8,128)}, u32[]{:S(2)}) copy-start(f32[4,128,128]{2,1,0:T(8,128)} %param.13) | copy-start | bytes 786436
  62.7 11.4 %all-to-all-start.1 = ((f32[3,4,16,128]{3,2,0,1:T(8,128)}), f32[3,4,16,128]{3,2,0,1:T(8,128)S(1)}, u32[]{:S(2)}, u32[]{:S(2)}) async-start(f32[3,4,16,128]{3,2,0,1:T(8,128)} %copy.102), calls=%async_computation.1 | async-start | bytes 196608 | tf_op jit(solution)/shard_map/all_to_all | solution.py:106
where the time goes:
time: 78.8 us; the launch traced here: 78.2 us
  starting transfers between devices  45.6 us (58%)
  waiting for transfers between devices  14 us (18%)
  other arithmetic  9.34 us (12%)
  local copies, waits for them, and re-layouts  7.94 us (10%)
  matrix products  0.96 us (1%)
    ppermute x4, starting transfers between devices, extended(): lax.ppermute(leading, axis, [(b, a) for a, b in up])  22.4 us
    ppermute x4, starting transfers between devices, extended(): lax.ppermute(last, axis, up)  13.1 us
    all_to_all x1, waiting for transfers between devices, local(): lax.all_to_all(restricted, 'group', split_axis=1, concat_axis=1, tiled=True)  5.8 us
    all_to_all x1, starting transfers between devices, local(): lax.all_to_all(restricted, 'group', split_axis=1, concat_axis=1, tiled=True)  5.63 us
    all_to_all x1, waiting for transfers between devices, local(): lax.all_to_all(picked, 'group', split_axis=1, concat_axis=1, tiled=True)  5.5 us
    all_to_all x1, starting transfers between devices, local(): lax.all_to_all(picked, 'group', split_axis=1, concat_axis=1, tiled=True)  4.46 us
    scatter-add x1, other arithmetic, local(): summed = jnp.zeros_like(blocks).at[:, parent_index].add(arrived.reshape(c...  2.74 us
    scatter-add x1, other arithmetic, local(): blocks.at[:, child_index].add(hanging)  2.73 us
  transfers between devices with their start and end apart: 10, of which 4 were waited for; matrix products, arithmetic and copies ran while one was open for 1% of the time, Pallas kernels for 0%

commit v1 on v0

v1 whole, which is shorter than its diff:
```python
import jax
import jax.numpy as jnp
from jax import lax
from jax.experimental import pallas as pl
from jax.experimental.pallas import tpu as pltpu
from jax.sharding import PartitionSpec as P

F32 = jnp.float32
BF16 = jnp.bfloat16
OMEGA = 2.0 / 3.0
THIRD = 1.0 / 3.0

PICK = 40
A_EDGE = 3 * PICK
A_PART = A_EDGE + 48
A_DIAG = A_PART + 48
A_CODE = A_DIAG + 16
A_ROWS = A_CODE + 8
B_PART = 96
B_DIAG = 192
B_CORN = 224
B_ROWS = 232

VMEM = pl.BlockSpec(memory_space=pltpu.VMEM)
SMEM = pl.BlockSpec(memory_space=pltpu.SMEM)


def z_pair(a):
    lane = lax.broadcasted_iota(jnp.int32, a.shape, a.ndim - 1)
    low = jnp.where(lane == 0, 0.0, pltpu.roll(a, 1, a.ndim - 1))
    high = jnp.where(lane == 127, 0.0, pltpu.roll(a, 127, a.ndim - 1))
    return low + high


def row_pair(a, before, after):
    n = a.shape[0]
    row = lax.broadcasted_iota(jnp.int32, a.shape, 0)
    low = jnp.where(row == 0, before, pltpu.roll(a, 1, 0))
    high = jnp.where(row == n - 1, after, pltpu.roll(a, n - 1, 0))
    return low + high


def split(a):
    high = a.astype(BF16)
    return high, (a - high.astype(F32)).astype(BF16)


def dot(a, b):
    return jnp.dot(a, b, preferred_element_type=F32)


def dot_t(a, b):
    return lax.dot_general(a, b, (((1,), (1,)), ((), ())), preferred_element_type=F32)


def filled_group(counts):
    target = jnp.int32(0)
    for d in range(1, 4):
        target = jnp.where(counts[0, 0, d] == 16, d, target)
    return target


def column(ref, c, y):
    return ref[c, pl.ds(y, 16, stride=32), :]


def pack(field, source, mass, parents, counts, children, kinds, out, rows):
    g = lax.axis_index("group")
    target = filled_group(counts)
    for d in range(5):
        for k in range(8):
            p = parents[0, 0, d, k] if d < 4 else parents[0, 0, target, 8 + k]
            for c in range(3):
                j = c * PICK + d * 8 + k
                rows[j : j + 1, :] = field[c, pl.ds(p, 1), :]
    slot = lax.broadcasted_iota(jnp.int32, (8, 128), 0)
    for d in range(5):
        live = slot < counts[0, 0, d] if d < 4 else slot + 8 < counts[0, 0, target]
        for c in range(3):
            at = c * PICK + d * 8
            part = jnp.where(live, rows[at : at + 8, :], 0.0)
            for p in range(4):
                out[p, at : at + 8, :] = part
    block = children[0, 0]
    y = block & 31
    x = block >> 5
    sides = []
    for edge, inner, depth in ((0, 1, y), (31, 30, 31 - y)):
        diag = OMEGA / (6.0 + mass[pl.ds(edge, 16, stride=32), :])
        firsts, parts = [], []
        for c in range(3):
            first = column(field, c, edge)
            beside = column(field, c, inner) + row_pair(first, 0.0, 0.0) + z_pair(first)
            firsts.append(first)
            parts.append(first * THIRD + diag * (column(source, c, edge) + beside))
        code = jnp.where(depth < 2, kinds[0, 0] * 32 + depth * 16 + x, -1)
        sides.append((firsts, parts, diag, code.astype(F32)))
    for p in range(4):
        right = p == g + 1
        for c in range(3):
            at = A_EDGE + 16 * c
            out[p, at : at + 16, :] = jnp.where(right, sides[1][0][c], sides[0][0][c])
            at = A_PART + 16 * c
            out[p, at : at + 16, :] = jnp.where(right, sides[1][1][c], sides[0][1][c])
        out[p, A_DIAG : A_DIAG + 16, :] = jnp.where(right, sides[1][2], sides[0][2])
        out[p, A_CODE : A_CODE + 8, :] = jnp.zeros((8, 128), F32)
        out[p, A_CODE : A_CODE + 4, 0:16] = jnp.where(right, sides[1][3], sides[0][3])


def lane_codes(rows):
    total = rows[0:1, :]
    for s in range(1, 4):
        total = total + pltpu.roll(rows[s : s + 1, :], 16 * s, 1)
    return total + pltpu.roll(total, 64, 1)


def selection(codes, start, count, stride):
    place = lax.broadcasted_iota(jnp.int32, (count, 128), 0) + start
    half = lax.broadcasted_iota(jnp.int32, (count, 128), 1) >> 6
    picked = []
    for pair in range(2):
        wanted = (place + (half + 2 * pair) * stride).astype(F32)
        picked.append(jnp.where(codes == wanted, 1.0, 0.0).astype(BF16))
    return jnp.concatenate(picked, axis=1)


def constrain(
    got, field, source, mass, interp, children, kinds, counts, cst, pay1, pay2, near, sweep, ndiag, codes
):
    g = lax.axis_index("group")
    odd = lax.axis_index("curve") & 1
    target = filled_group(counts)
    table = jnp.concatenate([interp[k] for k in range(4)], axis=1)
    table_h, table_l = split(table)

    def contributions(d):
        at = pl.multiple_of(d * 8, 8)
        rows = []
        for c in range(3):
            for s in range(4):
                rows.append(got[s, pl.ds(c * PICK + at, 8), :])
                more = got[s, c * PICK + 32 : c * PICK + 40, :]
                rows.append(jnp.where(target == d, more, 0.0))
        high, low = split(jnp.concatenate(rows, axis=0))
        product = dot(high, table_h) + dot(low, table_h) + dot(high, table_l)
        return split(
            jnp.concatenate(
                [
                    jnp.concatenate(
                        [product[64 * c : 64 * c + 64, 128 * k : 128 * k + 128] for c in range(3)], axis=1
                    )
                    for k in range(4)
                ],
                axis=0,
            )
        )

    codes[...] = jnp.zeros((8, 128), F32)
    codes[0:4, 0:16] = (kinds[0, 0] * 512 + children[0, 0]).astype(F32)
    own = lane_codes(codes)
    high, low = contributions(g)
    for q in range(4):
        chosen = selection(own, q * 128, 128, 512)
        added = dot(chosen, high) + dot(chosen, low)
        for c in range(3):
            rows = slice(q * 128, q * 128 + 128)
            cst[c, rows, :] = field[c, rows, :] + added[:, c * 128 : c * 128 + 128]

    for side in range(2):
        other = g - 1 if side == 0 else g + 1
        exists = (other >= 0) & (other < 4)
        s = jnp.clip(other, 0, 3)
        high, low = contributions(s)
        chosen = selection(lane_codes(got.at[s, A_CODE : A_CODE + 8, :]), 0, 32, 32)
        added = dot(chosen, high) + dot(chosen, low)
        diag = jnp.where(exists, got[s, A_DIAG : A_DIAG + 16, :], 0.0)
        ndiag[side] = diag
        for c in range(3):
            first = added[0:16, c * 128 : c * 128 + 128]
            second = added[16:32, c * 128 : c * 128 + 128]
            edge = got[s, A_EDGE + 16 * c : A_EDGE + 16 * c + 16, :] + first
            near[side, c] = jnp.where(exists, edge, 0.0)
            beside = second + row_pair(first, 0.0, 0.0) + z_pair(first)
            beside = beside + column(cst, c, 0 if side == 0 else 31)
            part = got[s, A_PART + 16 * c : A_PART + 16 * c + 16, :] + first * THIRD
            sweep[side, c] = jnp.where(exists, part + diag * beside, 0.0)

    for pay, upper in ((pay1, 1 - odd), (pay2, odd)):
        edge = upper * 15
        at = pl.multiple_of(edge * 32, 32)
        inner = pl.multiple_of((upper * 13 + 1) * 32, 32)
        diag = OMEGA / (6.0 + mass[pl.ds(at, 32), :])
        pay[B_DIAG : B_DIAG + 32, :] = diag
        pay[B_CORN : B_CORN + 8, :] = jnp.zeros((8, 128), F32)
        for c in range(3):
            first = cst[c, pl.ds(at, 32), :]
            left = near[0, c, pl.ds(edge, 1), :]
            right = near[1, c, pl.ds(edge, 1), :]
            beside = cst[c, pl.ds(inner, 32), :] + row_pair(first, left, right) + z_pair(first)
            pay[32 * c : 32 * c + 32, :] = first
            pay[B_PART + 32 * c : B_PART + 32 * c + 32, :] = first * THIRD + diag * (
                source[c, pl.ds(at, 32), :] + beside
            )
            pay[B_CORN + c : B_CORN + c + 1, :] = left
            pay[B_CORN + 3 + c : B_CORN + 4 + c, :] = right


def smooth(cst, source, mass, near, sweep, children, out, diag, chosen, mid):
    for x in range(16):
        rows = slice(32 * x, 32 * x + 32)
        diag[rows, :] = OMEGA / (6.0 + mass[rows, :])

    def step(state, halo, result):
        for x in range(16):
            rows = slice(32 * x, 32 * x + 32)
            d = diag[rows, :]
            for c in range(3):
                centre = state[c, rows, :]
                beside = row_pair(centre, halo[0, c, x : x + 1, :], halo[1, c, x : x + 1, :]) + z_pair(centre)
                if x > 0:
                    beside = beside + state[c, 32 * x - 32 : 32 * x, :]
                if x < 15:
                    beside = beside + state[c, 32 * x + 32 : 32 * x + 64, :]
                result[c, rows, :] = centre * THIRD + d * (source[c, rows, :] + beside)

    step(cst, near, mid)
    step(mid, sweep, out)
    for s in range(4):
        for k in range(16):
            b = children[0, 0, s, k]
            for c in range(3):
                j = s * 48 + c * 16 + k
                chosen[j : j + 1, :] = out[c, pl.ds(b, 1), :] - cst[c, pl.ds(b, 1), :]


def restrict(chosen, cst, diag, ndiag, got1, got2, interp, children, kinds, fix, out, placed):
    odd = lax.axis_index("curve") & 1
    placed[...] = jnp.zeros(placed.shape, F32)
    for got, upper in ((got1, 1 - odd), (got2, odd)):
        edge = upper * 15
        at = pl.multiple_of(edge * 32, 32)
        inner = pl.multiple_of((upper * 13 + 1) * 32, 32)
        d_edge = diag[pl.ds(at, 32), :]
        d_inner = diag[pl.ds(inner, 32), :]
        far = got[B_DIAG : B_DIAG + 32, :]
        for c in range(3):
            beyond = got[B_PART + 32 * c : B_PART + 32 * c + 32, :] + far * cst[c, pl.ds(at, 32), :]
            first = d_edge * got[32 * c : 32 * c + 32, :]
            left = ndiag[0, pl.ds(edge, 1), :] * got[B_CORN + c : B_CORN + c + 1, :]
            right = ndiag[1, pl.ds(edge, 1), :] * got[B_CORN + 3 + c : B_CORN + 4 + c, :]
            beside = beyond + row_pair(first, left, right) + z_pair(first)
            fix[c, pl.ds(pl.multiple_of(upper * 96, 32), 32), :] = first * THIRD + d_edge * beside
            fix[c, pl.ds(pl.multiple_of(upper * 32 + 32, 32), 32), :] = d_inner * first
    for c in range(3):
        fix[c, 128:136, :] = jnp.zeros((8, 128), F32)
    for s in range(4):
        for k in range(16):
            b = children[0, 0, s, k]
            kind = kinds[0, 0, s, k]
            spot = jnp.where(b < 64, b, jnp.where(b >= 448, b - 384, 128))
            for c in range(3):
                j = s * 48 + c * 16 + k
                placed[kind, pl.ds(j, 1), :] = chosen[j : j + 1, :] + fix[c, pl.ds(spot, 1), :]
    total = None
    for k in range(4):
        high, low = split(placed[k])
        table_h, table_l = split(interp[k])
        product = dot_t(high, table_h) + dot_t(low, table_h) + dot_t(high, table_l)
        total = product if total is None else total + product
    for s in range(4):
        out[s] = total[48 * s : 48 * s + 48, :]


def collect(state, fix, got, parents, counts, out, codes):
    codes[...] = jnp.zeros((8, 128), F32)
    slot = lax.broadcasted_iota(jnp.int32, (1, 16), 1)
    for d in range(4):
        codes[d : d + 1, 0:16] = jnp.where(
            slot < counts[0, 0, d], parents[0, 0, d : d + 1, :], -1
        ).astype(F32)
    total = codes[0:1, :]
    for s in range(1, 4):
        total = total + pltpu.roll(codes[s : s + 1, :], 16 * s, 1)
    rows = jnp.concatenate(
        [
            jnp.concatenate([got[d, 16 * c : 16 * c + 16, :] for d in range(4)], axis=0)
            for c in range(3)
        ],
        axis=1,
    )
    high, low = split(rows)
    place = lax.broadcasted_iota(jnp.int32, (128, 64), 0)
    for q in range(4):
        picked = jnp.where(total[:, 0:64] == (place + q * 128).astype(F32), 1.0, 0.0).astype(BF16)
        added = dot(picked, high) + dot(picked, low)
        for c in range(3):
            at = slice(q * 128, q * 128 + 128)
            result = state[c, at, :] + added[:, c * 128 : c * 128 + 128]
            if q == 0:
                result = jnp.concatenate([result[0:64] + fix[c, 0:64, :], result[64:128]], axis=0)
            if q == 3:
                result = jnp.concatenate([result[0:64], result[64:128] + fix[c, 64:128, :]], axis=0)
            out[c, at, :] = result


def shape(*dims):
    return jax.ShapeDtypeStruct(dims, F32)


def call(body, outs, ins, scratch=(), aliases=None, name=None, flops=1_000_000, moved=1_000_000, limit=16):
    many = isinstance(outs, list)
    return pl.pallas_call(
        body,
        out_shape=outs,
        in_specs=ins,
        out_specs=[VMEM] * len(outs) if many else VMEM,
        scratch_shapes=list(scratch),
        input_output_aliases=aliases or {},
        cost_estimate=pl.CostEstimate(flops=flops, bytes_accessed=moved, transcendentals=0),
        compiler_params=pltpu.CompilerParams(vmem_limit_bytes=limit << 20),
        name=name,
    )


def local(field, source, mass, interp, parents, children, kinds, counts):
    whole = field.shape
    field = field.reshape(3, 512, 128)
    source = source.reshape(3, 512, 128)
    mass = mass.reshape(512, 128)
    send = call(
        pack,
        shape(4, A_ROWS, 128),
        [VMEM, VMEM, VMEM, SMEM, SMEM, VMEM, VMEM],
        [pltpu.VMEM((3 * PICK, 128), F32)],
        name="pack",
    )(field, source, mass, parents, counts, children, kinds)
    got = lax.all_to_all(send, "group", 0, 0, tiled=True)
    cst, pay1, pay2, near, sweep, ndiag = call(
        constrain,
        [
            shape(3, 512, 128),
            shape(B_ROWS, 128),
            shape(B_ROWS, 128),
            shape(2, 3, 16, 128),
            shape(2, 3, 16, 128),
            shape(2, 16, 128),
        ],
        [VMEM] * 7 + [SMEM],
        [pltpu.VMEM((8, 128), F32)],
        name="constrain",
    )(got, field, source, mass, interp, children, kinds, counts)
    count = lax.axis_size("curve")
    inner = [(i, i ^ 1) for i in range(count)]
    outer = [(i, i + 1) for i in range(1, count - 1, 2)]
    outer = outer + [(b, a) for a, b in outer]
    got2 = lax.ppermute(pay2, "curve", outer)
    got1 = lax.ppermute(pay1, "curve", inner)
    state, diag, chosen = call(
        smooth,
        [shape(3, 512, 128), shape(512, 128), shape(192, 128)],
        [VMEM] * 5 + [SMEM],
        [pltpu.VMEM((3, 512, 128), F32)],
        name="smooth",
        flops=20_000_000,
        moved=8_000_000,
    )(cst, source, mass, near, sweep, children)
    fix, send = call(
        restrict,
        [shape(3, 136, 128), shape(4, 48, 128)],
        [VMEM] * 7 + [SMEM, SMEM],
        [pltpu.VMEM((4, 192, 128), F32)],
        name="restrict",
    )(chosen, cst, diag, ndiag, got1, got2, interp, children, kinds)
    got = lax.all_to_all(send, "group", 0, 0, tiled=True)
    out = call(
        collect,
        shape(3, 512, 128),
        [VMEM, VMEM, VMEM, VMEM, SMEM],
        [pltpu.VMEM((8, 128), F32)],
        name="collect",
    )(state, fix, got, parents, counts)
    return out.reshape(whole)


def solution(mesh):
    in_specs = (
        P(None, "curve", "group", None),
        P(None, "curve", "group", None),
        P("curve", "group", None),
        P(),
        P("curve", "group", None, None),
        P("curve", "group", None, None),
        P("curve", "group", None, None),
        P("curve", "group", None),
    )
    out_specs = P(None, "curve", "group", None)
    return jax.shard_map(local, mesh=mesh, in_specs=in_specs, out_specs=out_specs, check_vma=False)
```

time: 78.8 us -> 56.8 us (0.72)
  starting transfers between devices: 45.6 us -> 21 us
  blocking collectives: 0 us -> 21.7 us
  waiting for transfers between devices: 14 us -> 0.62 us
  other arithmetic: 9.34 us -> 0 us
  Pallas kernels: 0 us -> 7.75 us
  local copies, waits for them, and re-layouts: 7.94 us -> 5.28 us
  matrix products: 0.96 us -> 0 us
    all_to_all x0 -> x2, blocking collectives: none -> 21.7 us  [local(): got = lax.all_to_all(send, 'group', 0, 0, tiled=True)]
    ppermute x8 -> x2, starting transfers between devices: 35.5 us -> 21 us  [the longest x1 19 us: local(): got2 = lax.ppermute(pay2, 'curve', outer)]
    all_to_all x2 -> x0, waiting for transfers between devices: 11.3 us -> none  [the longest x1 5.8 us: local(): lax.all_to_all(restricted, 'group', split_axis=1, concat_axis=1, tiled=True)]
    all_to_all x2 -> x0, starting transfers between devices: 10.1 us -> none  [the longest x1 5.63 us: local(): lax.all_to_all(restricted, 'group', split_axis=1, concat_axis=1, tiled=True)]
    pallas_call x0 -> x5, Pallas kernels: none -> 7.75 us  [the longest x1 2.04 us: local(): call(constrain, [shape(3, 512, 128), shape(B_ROWS, 128), shape(B_ROWS, 12...]
    scatter-add x2 -> x0, other arithmetic: 5.47 us -> none  [the longest x1 2.74 us: local(): summed = jnp.zeros_like(blocks).at[:, parent_index].add(arrived.reshape(c...]
    unnamed x24 -> x20, local copies, waits for them, and re-layouts: 2.6 us -> 5.28 us
    ppermute x8 -> x2, waiting for transfers between devices: 2.73 us -> 0.62 us  [the longest x1 0.62 us: local(): got2 = lax.ppermute(pay2, 'curve', outer)]
  transfers between devices with their start and end apart: 10 -> 2, of which waited for: 4 -> 1; matrix products, arithmetic and copies ran while one was open for 1% -> 0% of each run, Pallas kernels for 0% -> 3%
where the time goes in v1:
time: 56.8 us; the launch traced here: 56.4 us
  blocking collectives  21.7 us (38%)
  starting transfers between devices  21 us (37%)
  Pallas kernels  7.75 us (14%)
  local copies, waits for them, and re-layouts  5.28 us (9%)
  waiting for transfers between devices  0.62 us (1%)
    all_to_all x2, blocking collectives, local(): got = lax.all_to_all(send, 'group', 0, 0, tiled=True)  21.7 us
    ppermute x1, starting transfers between devices, local(): got2 = lax.ppermute(pay2, 'curve', outer)  19 us
    unnamed x20, local copies, waits for them, and re-layouts  5.28 us
    pallas_call x1, Pallas kernels, local(): call(constrain, [shape(3, 512, 128), shape(B_ROWS, 128), shape(B_ROWS, 12...  2.04 us
    ppermute x1, starting transfers between devices, local(): got1 = lax.ppermute(pay1, 'curve', inner)  1.92 us
    pallas_call x1, Pallas kernels, local(): call(smooth, [shape(3, 512, 128), shape(512, 128), shape(192, 128)], [VME...  1.86 us
    pallas_call x1, Pallas kernels, local(): call(collect, shape(3, 512, 128), [VMEM, VMEM, VMEM, VMEM, SMEM], [pltpu....  1.84 us
    pallas_call x1, Pallas kernels, local(): call(restrict, [shape(3, 136, 128), shape(4, 48, 128)], [VMEM] * 7 + [SME...  1.25 us
  transfers between devices with their start and end apart: 2, of which 1 were waited for; matrix products, arithmetic and copies ran while one was open for 0% of the time, Pallas kernels for 3%

profile of v1, /device:TPU:6, one launch (start us, length us, event | category | flops | bytes accessed | tf_op | source)
XLA Modules:
  0.0 56.4 jit_solution(942515512690395123)
XLA Ops:
  0.0 0.0 copy-start.6
  0.0 0.0 copy-start.5
  0.0 0.7 %copy-done.6 = s32[1,1,4,16]{3,2,1,0:T(4,128)S(1)} copy-done((s32[1,1,4,16]{3,2,1,0:T(4,128)S(1)}, s32[1,1,4,16]{3,2,1,0:T(4,128)}, u32[]{:S(2)}) %copy-start.6) | copy-done | bytes 280
  0.7 0.0 copy-done.5
  0.7 0.0 copy-done.9
  0.7 1.1 %copy-done = f32[3,16,32,128]{3,2,1,0:T(8,128)S(1)} copy-done((f32[3,16,32,128]{3,2,1,0:T(8,128)S(1)}, f32[3,16,32,128]{3,2,1,0:T(8,128)}, u32[]{:S(2)}) %copy-start) | copy-done | bytes 786456
  1.8 1.1 %copy-done.2 = f32[3,16,32,128]{3,2,1,0:T(8,128)S(1)} copy-done((f32[3,16,32,128]{3,2,1,0:T(8,128)S(1)}, f32[3,16,32,128]{3,2,1,0:T(8,128)}, u32[]{:S(2)}) %copy-start.2) | copy-done | bytes 786456
  3.0 0.9 %copy-done.3 = f32[16,32,128]{2,1,0:T(8,128)S(1)} copy-done((f32[16,32,128]{2,1,0:T(8,128)S(1)}, f32[16,32,128]{2,1,0:T(8,128)}, u32[]{:S(2)}) %copy-start.3) | copy-done | bytes 262168
  3.9 0.7 %copy-done.7 = s32[1,1,4,16]{3,2,1,0:T(4,128)S(1)} copy-done((s32[1,1,4,16]{3,2,1,0:T(4,128)S(1)}, s32[1,1,4,16]{3,2,1,0:T(4,128)}, u32[]{:S(2)}) %copy-start.7) | copy-done | bytes 280
  4.6 0.8 %pack.1 = f32[4,240,128]{2,1,0:T(8,128)S(1)} custom-call(f32[3,512,128]{2,1,0:T(8,128)S(1)} %bitcast.7, f32[3,512,128]{2,1,0:T(8,128)S(1)} %bitcast.4, f32[512,128]{1,0:T(8,128)S(1)} %bitcast.9, s32[1,1,4,16]{3,2,1,0:T(4,128)S(1)} %copy-done.7, s32[1,1,4]{2,1,0:T(1,128)S(1)} %copy-done.9, s32[1,1,4,16]{3,2,1,0:T(4,128)S(1)} %copy-done.5, ...), custom_call_target="tpu_custom_call" | custom-call | flops 1000000 | bytes 1000000 | tf_op jit(solution)/shard_map/pack/pallas_call | solution.py:330
  5.4 0.0 copy-start.4
  5.4 13.5 %all_to_all.10.got = f32[4,240,128]{2,1,0:T(8,128)S(1)} all-to-all(f32[4,240,128]{2,1,0:T(8,128)S(1)} %pack.1), channel_id=1, replica_groups=mesh['curve'=256,'group'=4] {'group'}, dimensions={0} | all-to-all | bytes 983040 | tf_op jit(solution)/shard_map/all_to_all | solution.py:337
  18.9 0.0 copy-done.4
  18.9 2.0 %constrain.1 = (f32[3,512,128]{2,1,0:T(8,128)S(1)}, f32[232,128]{1,0:T(8,128)S(1)}, f32[232,128]{1,0:T(8,128)S(1)}, f32[2,3,16,128]{3,2,1,0:T(8,128)S(1)}, f32[2...) custom-call(f32[4,240,128]{2,1,0:T(8,128)S(1)} %all_to_all.10.got, f32[3,512,128]{2,1,0:T(8,128)S(1)} %bitcast.8, ...), custom_call_target="tpu_custom_call" | custom-call | flops 1000000 | bytes 1000000 | tf_op jit(solution)/shard_map/constrain/pallas_call | solution.py:338
  20.9 1.9 %collective-permute-start = (f32[232,128]{1,0:T(8,128)S(1)}, f32[232,128]{1,0:T(8,128)S(1)}, u32[]{:S(2)}, u32[]{:S(2)}) collective-permute-start(f32[232,128]{1,0:T(8,128)S(1)} %get-tuple-element.23), channel_id=1, source_target_pairs={{0,4},{4,0},{8,12},{12,8},{16,20},{20,16},{24,28},{28,24},{32,36},... | collective-permute-start | bytes 356360 | tf_op jit(solution)/shard_map/ppermute | solution.py:357
  22.9 19.0 %collective-permute-start.1 = (f32[232,128]{1,0:T(8,128)S(1)}, f32[232,128]{1,0:T(8,128)S(1)}, u32[]{:S(2)}, u32[]{:S(2)}) collective-permute-start(f32[232,128]{1,0:T(8,128)S(1)} %get-tuple-element.24), channel_id=1, source_target_pairs={{4,8},{12,16},{20,24},{28,32},{36,40},{44,48},{52,56},{60,64},{68,... | collective-permute-start | bytes 356360 | tf_op jit(solution)/shard_map/ppermute | solution.py:356
  41.9 0.0 copy-done.1
  41.9 1.9 %smooth.1 = (f32[3,512,128]{2,1,0:T(8,128)S(1)}, f32[512,128]{1,0:T(8,128)S(1)}, f32[192,128]{1,0:T(8,128)S(1)}) custom-call(f32[3,512,128]{2,1,0:T(8,128)S(1)} %get-tuple-element.16.cst, f32[3,512,128]{2,1,0:T(8,128)S(1)} %bitcast.6, f32[512,128]{1,0:T(8,128)S(1)} %bitcast.11, f32[2,3,16,128]{3,2,1,0:T(8,128)S(1)} %get-tuple-element.17.near, ...), custom_call_target="tpu_custom_call" | custom-call | flops 20000000 | bytes 8000000 | tf_op jit(solution)/shard_map/smooth/pallas_call | solution.py:358
  43.8 0.0 collective-permute-done.got1
  43.8 0.6 %collective-permute-done.1.got2 = f32[232,128]{1,0:T(8,128)S(1)} collective-permute-done((f32[232,128]{1,0:T(8,128)S(1)}, f32[232,128]{1,0:T(8,128)S(1)}, u32[]{:S(2)}, u32[]{:S(2)}) %collective-permute-start.1) | collective-permute-done | bytes 118816 | tf_op jit(solution)/shard_map/ppermute | solution.py:356
  44.4 1.3 %restrict.1 = (f32[3,136,128]{2,1,0:T(8,128)S(1)}, f32[4,48,128]{2,1,0:T(8,128)S(1)}) custom-call(f32[192,128]{1,0:T(8,128)S(1)} %get-tuple-element.20.chosen, f32[3,512,128]{2,1,0:T(8,128)S(1)} %get-tuple-element.16.cst, f32[512,128]{1,0:T(8,128)S(1)} %get-tuple-element.21.diag, f32[2,16,128]{2,1,0:T(8,128)S(1)} %get-tuple-element.22.ndiag, ...), custom_call_target="tpu_custom_call" | custom-call | flops 1000000 | bytes 1000000 | tf_op jit(solution)/shard_map/restrict/pallas_call | solution.py:367
  45.7 8.2 %all_to_all.11.got = f32[4,48,128]{2,1,0:T(8,128)S(1)} all-to-all(f32[4,48,128]{2,1,0:T(8,128)S(1)} %get-tuple-element.26), channel_id=1, replica_groups=mesh['curve'=256,'group'=4] {'group'}, dimensions={0} | all-to-all | bytes 196608 | tf_op jit(solution)/shard_map/all_to_all | solution.py:374
  53.9 0.7 %copy-done.8 = s32[1,1,4,16]{3,2,1,0:T(4,128)S(1)} copy-done((s32[1,1,4,16]{3,2,1,0:T(4,128)S(1)}, s32[1,1,4,16]{3,2,1,0:T(4,128)}, u32[]{:S(2)}) %copy-start.8) | copy-done | bytes 280
  54.5 1.8 %collect.1 = f32[3,512,128]{2,1,0:T(8,128)} custom-call(f32[3,512,128]{2,1,0:T(8,128)S(1)} %get-tuple-element.19.state, f32[3,136,128]{2,1,0:T(8,128)S(1)} %get-tuple-element.25.fix, f32[4,48,128]{2,1,0:T(8,128)S(1)} %all_to_all.11.got, s32[1,1,4,16]{3,2,1,0:T(4,128)S(1)} %copy-done.8, s32[1,1,4]{2,1,0:T(1,128)S(1)} %copy-done.9), custom_call_target="tpu_custom_call" | custom-call | flops 1000000 | bytes 1000000 | tf_op jit(solution)/shard_map/collect/pallas_call | solution.py:375
  (7 shorter events, 0.0 us)
Async XLA Ops:
  0.0 0.7 %copy-start.6 = (s32[1,1,4,16]{3,2,1,0:T(4,128)S(1)}, s32[1,1,4,16]{3,2,1,0:T(4,128)}, u32[]{:S(2)}) copy-start(s32[1,1,4,16]{3,2,1,0:T(4,128)} %kinds.5) | copy-start | bytes 772
  0.0 0.7 %copy-start.5 = (s32[1,1,4,16]{3,2,1,0:T(4,128)S(1)}, s32[1,1,4,16]{3,2,1,0:T(4,128)}, u32[]{:S(2)}) copy-start(s32[1,1,4,16]{3,2,1,0:T(4,128)} %children.7) | copy-start | bytes 772
  0.0 0.7 %copy-start.9 = (s32[1,1,4]{2,1,0:T(1,128)S(1)}, s32[1,1,4]{2,1,0:T(1,128)}, u32[]{:S(2)}) copy-start(s32[1,1,4]{2,1,0:T(1,128)} %counts.5) | copy-start | bytes 52
  0.7 1.1 %copy-start = (f32[3,16,32,128]{3,2,1,0:T(8,128)S(1)}, f32[3,16,32,128]{3,2,1,0:T(8,128)}, u32[]{:S(2)}) copy-start(f32[3,16,32,128]{3,2,1,0:T(8,128)} %param.9) | copy-start | bytes 2359300
  1.8 1.1 %copy-start.2 = (f32[3,16,32,128]{3,2,1,0:T(8,128)S(1)}, f32[3,16,32,128]{3,2,1,0:T(8,128)}, u32[]{:S(2)}) copy-start(f32[3,16,32,128]{3,2,1,0:T(8,128)} %param.8) | copy-start | bytes 2359300
  3.0 0.9 %copy-start.3 = (f32[16,32,128]{2,1,0:T(8,128)S(1)}, f32[16,32,128]{2,1,0:T(8,128)}, u32[]{:S(2)}) copy-start(f32[16,32,128]{2,1,0:T(8,128)} %param.10) | copy-start | bytes 786436
  3.9 0.7 %copy-start.7 = (s32[1,1,4,16]{3,2,1,0:T(4,128)S(1)}, s32[1,1,4,16]{3,2,1,0:T(4,128)}, u32[]{:S(2)}) copy-start(s32[1,1,4,16]{3,2,1,0:T(4,128)} %parents.3) | copy-start | bytes 772
  5.4 13.5 %copy-start.4 = (f32[4,128,128]{2,1,0:T(8,128)S(1)}, f32[4,128,128]{2,1,0:T(8,128)}, u32[]{:S(2)}) copy-start(f32[4,128,128]{2,1,0:T(8,128)} %interp.3) | copy-start | bytes 786436
  18.9 23.0 %copy-start.1 = (f32[3,16,32,128]{3,2,1,0:T(8,128)S(1)}, f32[3,16,32,128]{3,2,1,0:T(8,128)}, u32[]{:S(2)}) copy-start(f32[3,16,32,128]{3,2,1,0:T(8,128)} %param.9) | copy-start | bytes 2359300
  20.9 22.9 %collective-permute-start = (f32[232,128]{1,0:T(8,128)S(1)}, f32[232,128]{1,0:T(8,128)S(1)}, u32[]{:S(2)}, u32[]{:S(2)}) collective-permute-start(f32[232,128]{1,0:T(8,128)S(1)} %get-tuple-element.23), channel_id=1, source_target_pairs={{0,4},{4,0},{8,12},{12,8},{16,20},{20,16},{24,28},{28,24},{32,36},... | collective-permute-start | bytes 356360 | tf_op jit(solution)/shard_map/ppermute | solution.py:357
  22.9 21.6 %collective-permute-start.1 = (f32[232,128]{1,0:T(8,128)S(1)}, f32[232,128]{1,0:T(8,128)S(1)}, u32[]{:S(2)}, u32[]{:S(2)}) collective-permute-start(f32[232,128]{1,0:T(8,128)S(1)} %get-tuple-element.24), channel_id=1, source_target_pairs={{4,8},{12,16},{20,24},{28,32},{36,40},{44,48},{52,56},{60,64},{68,... | collective-permute-start | bytes 356360 | tf_op jit(solution)/shard_map/ppermute | solution.py:356
  53.9 0.7 %copy-start.8 = (s32[1,1,4,16]{3,2,1,0:T(4,128)S(1)}, s32[1,1,4,16]{3,2,1,0:T(4,128)}, u32[]{:S(2)}) copy-start(s32[1,1,4,16]{3,2,1,0:T(4,128)} %parents.3) | copy-start | bytes 772

commit v2 on v1

--- a/solution.py
+++ b/solution.py
@@ -5,12 +5,13 @@
 from jax.experimental.pallas import tpu as pltpu
 from jax.sharding import PartitionSpec as P
 
+
 F32 = jnp.float32
 BF16 = jnp.bfloat16
 OMEGA = 2.0 / 3.0
 THIRD = 1.0 / 3.0
 
-PICK = 40
+PICK = 32
 A_EDGE = 3 * PICK
 A_PART = A_EDGE + 48
 A_DIAG = A_PART + 48
@@ -23,6 +24,7 @@
 
 VMEM = pl.BlockSpec(memory_space=pltpu.VMEM)
 SMEM = pl.BlockSpec(memory_space=pltpu.SMEM)
+HBM = pl.BlockSpec(memory_space=pltpu.HBM)
 
 
 def z_pair(a):
@@ -64,36 +66,61 @@
     return ref[c, pl.ds(y, 16, stride=32), :]
 
 
-def pack(field, source, mass, parents, counts, children, kinds, out, rows):
+def pack(
+    field, source, mass, parents, counts, children, kinds, out, codes, f_all,
+    s_edge, m_edge, p_scalar, c_scalar, p_lane, child, kind, rows, sems,
+):
+    copies = [
+        pltpu.make_async_copy(parents, p_scalar, sems.at[0]),
+        pltpu.make_async_copy(counts, c_scalar, sems.at[1]),
+        pltpu.make_async_copy(field.at[0], f_all.at[0], sems.at[2]),
+        pltpu.make_async_copy(field.at[1], f_all.at[1], sems.at[3]),
+        pltpu.make_async_copy(field.at[2], f_all.at[2], sems.at[4]),
+        pltpu.make_async_copy(children, child, sems.at[5]),
+        pltpu.make_async_copy(kinds, kind, sems.at[6]),
+        pltpu.make_async_copy(parents, p_lane, sems.at[7]),
+        pltpu.make_async_copy(source.at[:, :, 0:8, :], s_edge.at[0], sems.at[8]),
+        pltpu.make_async_copy(source.at[:, :, 24:32, :], s_edge.at[1], sems.at[9]),
+        pltpu.make_async_copy(mass.at[:, 0:8, :], m_edge.at[0], sems.at[10]),
+        pltpu.make_async_copy(mass.at[:, 24:32, :], m_edge.at[1], sems.at[11]),
+    ]
+    for copy in copies:
+        copy.start()
     g = lax.axis_index("group")
-    target = filled_group(counts)
+    for copy in copies[:5]:
+        copy.wait()
+    target = filled_group(c_scalar)
     for d in range(5):
         for k in range(8):
-            p = parents[0, 0, d, k] if d < 4 else parents[0, 0, target, 8 + k]
+            p = p_scalar[0, 0, d, k] if d < 4 else p_scalar[0, 0, target, 8 + k]
             for c in range(3):
-                j = c * PICK + d * 8 + k
-                rows[j : j + 1, :] = field[c, pl.ds(p, 1), :]
+                j = c * 40 + d * 8 + k
+                rows[j : j + 1, :] = f_all[c, pl.ds(p, 1), :]
     slot = lax.broadcasted_iota(jnp.int32, (8, 128), 0)
     for d in range(5):
-        live = slot < counts[0, 0, d] if d < 4 else slot + 8 < counts[0, 0, target]
-        for c in range(3):
-            at = c * PICK + d * 8
+        live = slot < c_scalar[0, 0, d] if d < 4 else slot + 8 < c_scalar[0, 0, target]
+        for c in range(3):
+            at = c * 40 + d * 8
             part = jnp.where(live, rows[at : at + 8, :], 0.0)
             for p in range(4):
-                out[p, at : at + 8, :] = part
-    block = children[0, 0]
+                near = 3 if d == 4 else d - p + 1
+                if 0 <= near < 4 and (d == 4 or near < 3):
+                    out[p, c * PICK + near * 8 : c * PICK + near * 8 + 8, :] = part
+    for copy in copies[5:]:
+        copy.wait()
+    block = child[0, 0]
     y = block & 31
     x = block >> 5
     sides = []
-    for edge, inner, depth in ((0, 1, y), (31, 30, 31 - y)):
-        diag = OMEGA / (6.0 + mass[pl.ds(edge, 16, stride=32), :])
+    for side, edge, inner, depth in ((0, 0, 1, y), (1, 31, 30, 31 - y)):
+        diag = OMEGA / (6.0 + m_edge[side, :, 7 * side, :])
         firsts, parts = [], []
         for c in range(3):
-            first = column(field, c, edge)
-            beside = column(field, c, inner) + row_pair(first, 0.0, 0.0) + z_pair(first)
+            first = column(f_all, c, edge)
+            beside = column(f_all, c, inner) + row_pair(first, 0.0, 0.0) + z_pair(first)
             firsts.append(first)
-            parts.append(first * THIRD + diag * (column(source, c, edge) + beside))
-        code = jnp.where(depth < 2, kinds[0, 0] * 32 + depth * 16 + x, -1)
+            parts.append(first * THIRD + diag * (s_edge[side, c, :, 7 * side, :] + beside))
+        code = jnp.where(depth < 2, kind[0, 0] * 32 + depth * 16 + x, -1)
         sides.append((firsts, parts, diag, code.astype(F32)))
     for p in range(4):
         right = p == g + 1
@@ -105,6 +132,10 @@
         out[p, A_DIAG : A_DIAG + 16, :] = jnp.where(right, sides[1][2], sides[0][2])
         out[p, A_CODE : A_CODE + 8, :] = jnp.zeros((8, 128), F32)
         out[p, A_CODE : A_CODE + 4, 0:16] = jnp.where(right, sides[1][3], sides[0][3])
+    codes[...] = jnp.zeros((8, 128), F32)
+    slots = lax.broadcasted_iota(jnp.int32, (1, 16), 1)
+    for d in range(4):
+        codes[d : d + 1, 0:16] = jnp.where(slots < c_scalar[0, 0, d], p_lane[0, 0, d : d + 1, :], -1).astype(F32)
 
 
 def lane_codes(rows):
@@ -133,13 +164,12 @@
     table = jnp.concatenate([interp[k] for k in range(4)], axis=1)
     table_h, table_l = split(table)
 
-    def contributions(d):
-        at = pl.multiple_of(d * 8, 8)
+    def contributions(d, near):
         rows = []
         for c in range(3):
             for s in range(4):
-                rows.append(got[s, pl.ds(c * PICK + at, 8), :])
-                more = got[s, c * PICK + 32 : c * PICK + 40, :]
+                rows.append(got[s, c * PICK + near * 8 : c * PICK + near * 8 + 8, :])
+                more = got[s, c * PICK + 24 : c * PICK + 32, :]
                 rows.append(jnp.where(target == d, more, 0.0))
         high, low = split(jnp.concatenate(rows, axis=0))
         product = dot(high, table_h) + dot(low, table_h) + dot(high, table_l)
@@ -158,7 +188,7 @@
     codes[...] = jnp.zeros((8, 128), F32)
     codes[0:4, 0:16] = (kinds[0, 0] * 512 + children[0, 0]).astype(F32)
     own = lane_codes(codes)
-    high, low = contributions(g)
+    high, low = contributions(g, 1)
     for q in range(4):
         chosen = selection(own, q * 128, 128, 512)
         added = dot(chosen, high) + dot(chosen, low)
@@ -170,7 +200,7 @@
         other = g - 1 if side == 0 else g + 1
         exists = (other >= 0) & (other < 4)
         s = jnp.clip(other, 0, 3)
-        high, low = contributions(s)
+        high, low = contributions(s, 2 * side)
         chosen = selection(lane_codes(got.at[s, A_CODE : A_CODE + 8, :]), 0, 32, 32)
         added = dot(chosen, high) + dot(chosen, low)
         diag = jnp.where(exists, got[s, A_DIAG : A_DIAG + 16, :], 0.0)
@@ -271,13 +301,7 @@
         out[s] = total[48 * s : 48 * s + 48, :]
 
 
-def collect(state, fix, got, parents, counts, out, codes):
-    codes[...] = jnp.zeros((8, 128), F32)
-    slot = lax.broadcasted_iota(jnp.int32, (1, 16), 1)
-    for d in range(4):
-        codes[d : d + 1, 0:16] = jnp.where(
-            slot < counts[0, 0, d], parents[0, 0, d : d + 1, :], -1
-        ).astype(F32)
+def collect(state, fix, got, codes, out, result, sems):
     total = codes[0:1, :]
     for s in range(1, 4):
         total = total + pltpu.roll(codes[s : s + 1, :], 16 * s, 1)
@@ -290,50 +314,67 @@
     )
     high, low = split(rows)
     place = lax.broadcasted_iota(jnp.int32, (128, 64), 0)
+    copies = []
     for q in range(4):
         picked = jnp.where(total[:, 0:64] == (place + q * 128).astype(F32), 1.0, 0.0).astype(BF16)
         added = dot(picked, high) + dot(picked, low)
         for c in range(3):
             at = slice(q * 128, q * 128 + 128)
-            result = state[c, at, :] + added[:, c * 128 : c * 128 + 128]
+            final = state[c, at, :] + added[:, c * 128 : c * 128 + 128]
             if q == 0:
-                result = jnp.concatenate([result[0:64] + fix[c, 0:64, :], result[64:128]], axis=0)
+                final = jnp.concatenate([final[0:64] + fix[c, 0:64, :], final[64:128]], axis=0)
             if q == 3:
-                result = jnp.concatenate([result[0:64], result[64:128] + fix[c, 64:128, :]], axis=0)
-            out[c, at, :] = result
+                final = jnp.concatenate([final[0:64], final[64:128] + fix[c, 64:128, :]], axis=0)
+            result[c, at, :] = final
+            copy = pltpu.make_async_copy(result.at[c, at, :], out.at[c, at, :], sems.at[len(copies)])
+            copy.start()
+            copies.append(copy)
+    for copy in copies:
+        copy.wait()
+
+
+def stay(array):
+    return pltpu.with_memory_space_constraint(array, pltpu.HBM)
 
 
 def shape(*dims):
     return jax.ShapeDtypeStruct(dims, F32)
 
 
-def call(body, outs, ins, scratch=(), aliases=None, name=None, flops=1_000_000, moved=1_000_000, limit=16):
+def call(body, outs, ins, scratch=(), aliases=None, to=VMEM, flops=1_000_000, moved=1_000_000, limit=16384):
     many = isinstance(outs, list)
     return pl.pallas_call(
         body,
         out_shape=outs,
         in_specs=ins,
-        out_specs=[VMEM] * len(outs) if many else VMEM,
+        out_specs=[to] * len(outs) if many else to,
         scratch_shapes=list(scratch),
         input_output_aliases=aliases or {},
         cost_estimate=pl.CostEstimate(flops=flops, bytes_accessed=moved, transcendentals=0),
-        compiler_params=pltpu.CompilerParams(vmem_limit_bytes=limit << 20),
-        name=name,
+        compiler_params=pltpu.CompilerParams(vmem_limit_bytes=limit << 10),
     )
 
 
 def local(field, source, mass, interp, parents, children, kinds, counts):
     whole = field.shape
-    field = field.reshape(3, 512, 128)
+    send, codes, field = call(
+        pack,
+        [shape(4, A_ROWS, 128), shape(8, 128), shape(3, 512, 128)],
+        [HBM] * 7,
+        [
+            pltpu.VMEM((2, 3, 16, 8, 128), F32),
+            pltpu.VMEM((2, 16, 8, 128), F32),
+            pltpu.SMEM(parents.shape, jnp.int32),
+            pltpu.SMEM(counts.shape, jnp.int32),
+            pltpu.VMEM(parents.shape, jnp.int32),
+            pltpu.VMEM(parents.shape, jnp.int32),
+            pltpu.VMEM(parents.shape, jnp.int32),
+            pltpu.VMEM((120, 128), F32),
+            pltpu.SemaphoreType.DMA((12,)),
+        ],
+    )(*map(stay, (field.reshape(3, 512, 128), source, mass, parents, counts, children, kinds)))
     source = source.reshape(3, 512, 128)
     mass = mass.reshape(512, 128)
-    send = call(
-        pack,
-        shape(4, A_ROWS, 128),
-        [VMEM, VMEM, VMEM, SMEM, SMEM, VMEM, VMEM],
-        [pltpu.VMEM((3 * PICK, 128), F32)],
-        name="pack",
-    )(field, source, mass, parents, counts, children, kinds)
     got = lax.all_to_all(send, "group", 0, 0, tiled=True)
     cst, pay1, pay2, near, sweep, ndiag = call(
         constrain,
@@ -347,7 +388,6 @@
         ],
         [VMEM] * 7 + [SMEM],
         [pltpu.VMEM((8, 128), F32)],
-        name="constrain",
     )(got, field, source, mass, interp, children, kinds, counts)
     count = lax.axis_size("curve")
     inner = [(i, i ^ 1) for i in range(count)]
@@ -360,7 +400,6 @@
         [shape(3, 512, 128), shape(512, 128), shape(192, 128)],
         [VMEM] * 5 + [SMEM],
         [pltpu.VMEM((3, 512, 128), F32)],
-        name="smooth",
         flops=20_000_000,
         moved=8_000_000,
     )(cst, source, mass, near, sweep, children)
@@ -369,16 +408,15 @@
         [shape(3, 136, 128), shape(4, 48, 128)],
         [VMEM] * 7 + [SMEM, SMEM],
         [pltpu.VMEM((4, 192, 128), F32)],
-        name="restrict",
     )(chosen, cst, diag, ndiag, got1, got2, interp, children, kinds)
     got = lax.all_to_all(send, "group", 0, 0, tiled=True)
     out = call(
         collect,
         shape(3, 512, 128),
-        [VMEM, VMEM, VMEM, VMEM, SMEM],
-        [pltpu.VMEM((8, 128), F32)],
-        name="collect",
-    )(state, fix, got, parents, counts)
+        [VMEM] * 4,
+        [pltpu.VMEM((3, 512, 128), F32), pltpu.SemaphoreType.DMA((12,))],
+        to=HBM,
+    )(state, fix, got, codes)
     return out.reshape(whole)
 
 

time: 56.8 us -> 51.8 us (0.912)
  local copies, waits for them, and re-layouts: 5.28 us -> 0.69 us
    unnamed x20 -> x12, local copies, waits for them, and re-layouts: 5.28 us -> 0.69 us
  transfers between devices with their start and end apart: 2 -> 2, of which waited for: 1 -> 1; matrix products, arithmetic and copies ran while one was open for 0% -> 0% of each run, Pallas kernels for 3% -> 4%
where the time goes in v2:
time: 51.8 us; the launch traced here: 51.5 us
  blocking collectives  21.2 us (41%)
  starting transfers between devices  21 us (41%)
  Pallas kernels  8 us (15%)
  local copies, waits for them, and re-layouts  0.69 us (1%)
  waiting for transfers between devices  0.63 us (1%)
    all_to_all x2, blocking collectives, local(): got = lax.all_to_all(send, 'group', 0, 0, tiled=True)  21.2 us
    ppermute x1, starting transfers between devices, local(): got2 = lax.ppermute(pay2, 'curve', outer)  19.1 us
    pallas_call x1, Pallas kernels, local(): call(constrain, [shape(3, 512, 128), shape(B_ROWS, 128), shape(B_ROWS, 12...  2.03 us
    ppermute x1, starting transfers between devices, local(): got1 = lax.ppermute(pay1, 'curve', inner)  1.92 us
    pallas_call x1, Pallas kernels, local(): call(smooth, [shape(3, 512, 128), shape(512, 128), shape(192, 128)], [VME...  1.86 us
    pallas_call x1, Pallas kernels, local(): call(pack, [shape(4, A_ROWS, 128), shape(8, 128), shape(3, 512, 128)], [H...  1.61 us
    pallas_call x1, Pallas kernels, local(): call(restrict, [shape(3, 136, 128), shape(4, 48, 128)], [VMEM] * 7 + [SME...  1.26 us
    pallas_call x1, Pallas kernels, local(): call(collect, shape(3, 512, 128), [VMEM] * 4, [pltpu.VMEM((3, 512, 128),...  1.25 us
  transfers between devices with their start and end apart: 2, of which 1 were waited for; matrix products, arithmetic and copies ran while one was open for 0% of the time, Pallas kernels for 4%

profile of v2, /device:TPU:6, one launch (start us, length us, event | category | flops | bytes accessed | tf_op | source)
XLA Modules:
  0.0 51.5 jit_solution(3569097871106489950)
XLA Ops:
  0.0 0.0 copy-start.1
  0.0 0.0 copy-start.2
  0.0 1.6 %shard_map.82 = (f32[4,216,128]{2,1,0:T(8,128)S(1)}, f32[8,128]{1,0:T(8,128)S(1)}, f32[3,512,128]{2,1,0:T(8,128)S(1)}) custom-call(f32[3,512,128]{2,1,0:T(8,128)} %bitcast.8, f32[3,16,32,128]{3,2,1,0:T(8,128)} %source.1, f32[16,32,128]{2,1,0:T(8,128)} %mass.1, s32[1,1,4,16]{3,2,1,0:T(4,128)} %parents.1, s32[1,1,4]{2,1,0:T(1,128)} %counts.3, ...), custom_call_target="tpu_custom_call" | custom-call | flops 1000000 | bytes 1000000 | tf_op jit(solution)/shard_map/pallas_call | solution.py:360
  1.6 0.0 copy-start
  1.6 13.0 %all_to_all.10.got = f32[4,216,128]{2,1,0:T(8,128)S(1)} all-to-all(f32[4,216,128]{2,1,0:T(8,128)S(1)} %get-tuple-element.19), channel_id=1, replica_groups=mesh['curve'=256,'group'=4] {'group'}, dimensions={0} | all-to-all | bytes 884736 | tf_op jit(solution)/shard_map/all_to_all | solution.py:378
  14.6 0.0 copy-start.4
  14.6 0.0 copy-start.3
  14.6 0.0 copy-start.5
  14.6 0.0 copy-done.1
  14.6 0.0 copy-done.2
  14.7 0.0 copy-done
  14.7 0.7 %copy-done.4 = s32[1,1,4,16]{3,2,1,0:T(4,128)S(1)} copy-done((s32[1,1,4,16]{3,2,1,0:T(4,128)S(1)}, s32[1,1,4,16]{3,2,1,0:T(4,128)}, u32[]{:S(2)}) %copy-start.4) | copy-done | bytes 280
  15.3 0.0 copy-done.3
  15.3 0.0 copy-done.5
  15.3 2.0 %shard_map.83 = (f32[3,512,128]{2,1,0:T(8,128)S(1)}, f32[232,128]{1,0:T(8,128)S(1)}, f32[232,128]{1,0:T(8,128)S(1)}, f32[2,3,16,128]{3,2,1,0:T(8,128)S(1)}, f32[...) custom-call(f32[4,216,128]{2,1,0:T(8,128)S(1)} %all_to_all.10.got, f32[3,512,128]{2,1,0:T(8,128)S(1)} %get-tuple-element.20.field, ...), custom_call_target="tpu_custom_call" | custom-call | flops 1000000 | bytes 1000000 | tf_op jit(solution)/shard_map/pallas_call | solution.py:379
  17.4 1.9 %collective-permute-start = (f32[232,128]{1,0:T(8,128)S(1)}, f32[232,128]{1,0:T(8,128)S(1)}, u32[]{:S(2)}, u32[]{:S(2)}) collective-permute-start(f32[232,128]{1,0:T(8,128)S(1)} %get-tuple-element.28), channel_id=1, source_target_pairs={{0,4},{4,0},{8,12},{12,8},{16,20},{20,16},{24,28},{28,24},{32,36},... | collective-permute-start | bytes 356360 | tf_op jit(solution)/shard_map/ppermute | solution.py:397
  19.3 19.1 %collective-permute-start.1 = (f32[232,128]{1,0:T(8,128)S(1)}, f32[232,128]{1,0:T(8,128)S(1)}, u32[]{:S(2)}, u32[]{:S(2)}) collective-permute-start(f32[232,128]{1,0:T(8,128)S(1)} %get-tuple-element.29), channel_id=1, source_target_pairs={{4,8},{12,16},{20,24},{28,32},{36,40},{44,48},{52,56},{60,64},{68,... | collective-permute-start | bytes 356360 | tf_op jit(solution)/shard_map/ppermute | solution.py:396
  38.4 1.9 %shard_map.84 = (f32[3,512,128]{2,1,0:T(8,128)S(1)}, f32[512,128]{1,0:T(8,128)S(1)}, f32[192,128]{1,0:T(8,128)S(1)}) custom-call(f32[3,512,128]{2,1,0:T(8,128)S(1)} %get-tuple-element.21.cst, f32[3,512,128]{2,1,0:T(8,128)S(1)} %bitcast.5, f32[512,128]{1,0:T(8,128)S(1)} %bitcast.7, f32[2,3,16,128]{3,2,1,0:T(8,128)S(1)} %get-tuple-element.22.near, ...), custom_call_target="tpu_custom_call" | custom-call | flops 20000000 | bytes 8000000 | tf_op jit(solution)/shard_map/pallas_call | solution.py:398
  40.2 0.0 collective-permute-done.got1
  40.2 0.6 %collective-permute-done.1.got2 = f32[232,128]{1,0:T(8,128)S(1)} collective-permute-done((f32[232,128]{1,0:T(8,128)S(1)}, f32[232,128]{1,0:T(8,128)S(1)}, u32[]{:S(2)}, u32[]{:S(2)}) %collective-permute-start.1) | collective-permute-done | bytes 118816 | tf_op jit(solution)/shard_map/ppermute | solution.py:396
  40.9 1.3 %shard_map.85 = (f32[3,136,128]{2,1,0:T(8,128)S(1)}, f32[4,48,128]{2,1,0:T(8,128)S(1)}) custom-call(f32[192,128]{1,0:T(8,128)S(1)} %get-tuple-element.25.chosen, f32[3,512,128]{2,1,0:T(8,128)S(1)} %get-tuple-element.21.cst, f32[512,128]{1,0:T(8,128)S(1)} %get-tuple-element.26.diag, f32[2,16,128]{2,1,0:T(8,128)S(1)} %get-tuple-element.27.ndiag, ...), custom_call_target="tpu_custom_call" | custom-call | flops 1000000 | bytes 1000000 | tf_op jit(solution)/shard_map/pallas_call | solution.py:406
  42.1 8.2 %all_to_all.11.got = f32[4,48,128]{2,1,0:T(8,128)S(1)} all-to-all(f32[4,48,128]{2,1,0:T(8,128)S(1)} %get-tuple-element.31), channel_id=1, replica_groups=mesh['curve'=256,'group'=4] {'group'}, dimensions={0} | all-to-all | bytes 196608 | tf_op jit(solution)/shard_map/all_to_all | solution.py:412
  50.3 1.2 %shard_map.86 = f32[3,512,128]{2,1,0:T(8,128)} custom-call(f32[3,512,128]{2,1,0:T(8,128)S(1)} %get-tuple-element.24.state, f32[3,136,128]{2,1,0:T(8,128)S(1)} %get-tuple-element.30.fix, f32[4,48,128]{2,1,0:T(8,128)S(1)} %all_to_all.11.got, f32[8,128]{1,0:T(8,128)S(1)} %get-tuple-element.32.codes), custom_call_target="tpu_custom_call" | custom-call | flops 1000000 | bytes 1000000 | tf_op jit(solution)/shard_map/pallas_call | solution.py:413
Async XLA Ops:
  0.0 14.6 %copy-start.1 = (f32[16,32,128]{2,1,0:T(8,128)S(1)}, f32[16,32,128]{2,1,0:T(8,128)}, u32[]{:S(2)}) copy-start(f32[16,32,128]{2,1,0:T(8,128)} %mass.1) | copy-start | bytes 786436
  0.0 14.6 %copy-start.2 = (f32[4,128,128]{2,1,0:T(8,128)S(1)}, f32[4,128,128]{2,1,0:T(8,128)}, u32[]{:S(2)}) copy-start(f32[4,128,128]{2,1,0:T(8,128)} %interp.3) | copy-start | bytes 786436
  1.6 13.0 %copy-start = (f32[3,16,32,128]{3,2,1,0:T(8,128)S(1)}, f32[3,16,32,128]{3,2,1,0:T(8,128)}, u32[]{:S(2)}) copy-start(f32[3,16,32,128]{3,2,1,0:T(8,128)} %source.1) | copy-start | bytes 2359300
  14.6 0.7 %copy-start.4 = (s32[1,1,4,16]{3,2,1,0:T(4,128)S(1)}, s32[1,1,4,16]{3,2,1,0:T(4,128)}, u32[]{:S(2)}) copy-start(s32[1,1,4,16]{3,2,1,0:T(4,128)} %kinds.5) | copy-start | bytes 772
  14.6 0.7 %copy-start.3 = (s32[1,1,4,16]{3,2,1,0:T(4,128)S(1)}, s32[1,1,4,16]{3,2,1,0:T(4,128)}, u32[]{:S(2)}) copy-start(s32[1,1,4,16]{3,2,1,0:T(4,128)} %children.7) | copy-start | bytes 772
  14.6 0.7 %copy-start.5 = (s32[1,1,4]{2,1,0:T(1,128)S(1)}, s32[1,1,4]{2,1,0:T(1,128)}, u32[]{:S(2)}) copy-start(s32[1,1,4]{2,1,0:T(1,128)} %counts.3) | copy-start | bytes 52
  17.4 22.9 %collective-permute-start = (f32[232,128]{1,0:T(8,128)S(1)}, f32[232,128]{1,0:T(8,128)S(1)}, u32[]{:S(2)}, u32[]{:S(2)}) collective-permute-start(f32[232,128]{1,0:T(8,128)S(1)} %get-tuple-element.28), channel_id=1, source_target_pairs={{0,4},{4,0},{8,12},{12,8},{16,20},{20,16},{24,28},{28,24},{32,36},... | collective-permute-start | bytes 356360 | tf_op jit(solution)/shard_map/ppermute | solution.py:397
  19.3 21.6 %collective-permute-start.1 = (f32[232,128]{1,0:T(8,128)S(1)}, f32[232,128]{1,0:T(8,128)S(1)}, u32[]{:S(2)}, u32[]{:S(2)}) collective-permute-start(f32[232,128]{1,0:T(8,128)S(1)} %get-tuple-element.29), channel_id=1, source_target_pairs={{4,8},{12,16},{20,24},{28,32},{36,40},{44,48},{52,56},{60,64},{68,... | collective-permute-start | bytes 356360 | tf_op jit(solution)/shard_map/ppermute | solution.py:396

commit v3 on v2

v3 whole, which is shorter than its diff:
```python
import functools

import jax
import jax.numpy as jnp
from jax import lax
from jax.experimental import pallas as pl
from jax.experimental.pallas import tpu as pltpu
from jax.sharding import PartitionSpec as P


F32 = jnp.float32
BF16 = jnp.bfloat16
OMEGA = 2.0 / 3.0
THIRD = 1.0 / 3.0

PICK = 32
A_EDGE = 3 * PICK
A_PART = A_EDGE + 48
A_DIAG = A_PART + 48
A_CODE = A_DIAG + 16
A_ROWS = A_CODE + 8
B_PART = 96
B_DIAG = 192
B_CORN = 224
B_ROWS = 232

VMEM = pl.BlockSpec(memory_space=pltpu.VMEM)
SMEM = pl.BlockSpec(memory_space=pltpu.SMEM)
HBM = pl.BlockSpec(memory_space=pltpu.HBM)


def z_pair(a):
    lane = lax.broadcasted_iota(jnp.int32, a.shape, a.ndim - 1)
    low = jnp.where(lane == 0, 0.0, pltpu.roll(a, 1, a.ndim - 1))
    high = jnp.where(lane == 127, 0.0, pltpu.roll(a, 127, a.ndim - 1))
    return low + high


def row_pair(a, before, after):
    n = a.shape[0]
    row = lax.broadcasted_iota(jnp.int32, a.shape, 0)
    low = jnp.where(row == 0, before, pltpu.roll(a, 1, 0))
    high = jnp.where(row == n - 1, after, pltpu.roll(a, n - 1, 0))
    return low + high


def split(a):
    high = a.astype(BF16)
    return high, (a - high.astype(F32)).astype(BF16)


def dot(a, b):
    return jnp.dot(a, b, preferred_element_type=F32)


def dot_t(a, b):
    return lax.dot_general(a, b, (((1,), (1,)), ((), ())), preferred_element_type=F32)


def filled_group(counts):
    target = jnp.int32(0)
    for d in range(1, 4):
        target = jnp.where(counts[0, 0, d] == 16, d, target)
    return target


def column(ref, c, y):
    return ref[c, pl.ds(y, 16, stride=32), :]


def pack(
    field, source, mass, parents, counts, children, kinds, out, codes, f_all,
    s_edge, m_edge, p_scalar, c_scalar, p_lane, child, kind, rows, sems,
):
    copies = [
        pltpu.make_async_copy(parents, p_scalar, sems.at[0]),
        pltpu.make_async_copy(counts, c_scalar, sems.at[1]),
        pltpu.make_async_copy(field.at[0], f_all.at[0], sems.at[2]),
        pltpu.make_async_copy(field.at[1], f_all.at[1], sems.at[3]),
        pltpu.make_async_copy(field.at[2], f_all.at[2], sems.at[4]),
        pltpu.make_async_copy(children, child, sems.at[5]),
        pltpu.make_async_copy(kinds, kind, sems.at[6]),
        pltpu.make_async_copy(parents, p_lane, sems.at[7]),
        pltpu.make_async_copy(source.at[:, :, 0:8, :], s_edge.at[0], sems.at[8]),
        pltpu.make_async_copy(source.at[:, :, 24:32, :], s_edge.at[1], sems.at[9]),
        pltpu.make_async_copy(mass.at[:, 0:8, :], m_edge.at[0], sems.at[10]),
        pltpu.make_async_copy(mass.at[:, 24:32, :], m_edge.at[1], sems.at[11]),
    ]
    for copy in copies:
        copy.start()
    g = lax.axis_index("group")
    for copy in (copies[0], copies[1], *copies[5:8]):
        copy.wait()
    target = filled_group(c_scalar)
    slots = lax.broadcasted_iota(jnp.int32, (1, 16), 1)
    codes[...] = jnp.zeros((24, 128), F32)
    for d in range(4):
        codes[d : d + 1, 0:16] = jnp.where(slots < c_scalar[0, 0, d], p_lane[0, 0, d : d + 1, :], -1).astype(F32)
    codes[8:12, 0:16] = (kind[0, 0] * 512 + child[0, 0]).astype(F32)
    for at in (0, 8):
        codes[at : at + 1, :] = lane_codes(codes.at[at : at + 8, :])
    codes[16:24, :] = jnp.full((8, 128), target.astype(F32))
    for copy in copies[2:5]:
        copy.wait()
    for d in range(5):
        for k in range(8):
            p = p_scalar[0, 0, d, k] if d < 4 else p_scalar[0, 0, target, 8 + k]
            for c in range(3):
                j = c * 40 + d * 8 + k
                rows[j : j + 1, :] = f_all[c, pl.ds(p, 1), :]
    slot = lax.broadcasted_iota(jnp.int32, (8, 128), 0)
    for d in range(5):
        live = slot < c_scalar[0, 0, d] if d < 4 else slot + 8 < c_scalar[0, 0, target]
        for c in range(3):
            at = c * 40 + d * 8
            part = jnp.where(live, rows[at : at + 8, :], 0.0)
            for p in range(4):
                near = 3 if d == 4 else d - p + 1
                if 0 <= near < 4 and (d == 4 or near < 3):
                    out[p, c * PICK + near * 8 : c * PICK + near * 8 + 8, :] = part
    for copy in copies[8:]:
        copy.wait()
    block = child[0, 0]
    y = block & 31
    x = block >> 5
    sides = []
    for side, edge, inner, depth in ((0, 0, 1, y), (1, 31, 30, 31 - y)):
        diag = OMEGA / (6.0 + m_edge[side, :, 7 * side, :])
        firsts, parts = [], []
        for c in range(3):
            first = column(f_all, c, edge)
            beside = column(f_all, c, inner) + row_pair(first, 0.0, 0.0) + z_pair(first)
            firsts.append(first)
            parts.append(first * THIRD + diag * (s_edge[side, c, :, 7 * side, :] + beside))
        code = jnp.where(depth < 2, kind[0, 0] * 32 + depth * 16 + x, -1)
        sides.append((firsts, parts, diag, code.astype(F32)))
    for p in range(4):
        right = p == g + 1
        for c in range(3):
            at = A_EDGE + 16 * c
            out[p, at : at + 16, :] = jnp.where(right, sides[1][0][c], sides[0][0][c])
            at = A_PART + 16 * c
            out[p, at : at + 16, :] = jnp.where(right, sides[1][1][c], sides[0][1][c])
        out[p, A_DIAG : A_DIAG + 16, :] = jnp.where(right, sides[1][2], sides[0][2])
        out[p, A_CODE : A_CODE + 8, :] = jnp.zeros((8, 128), F32)
        out[p, A_CODE : A_CODE + 4, 0:16] = jnp.where(right, sides[1][3], sides[0][3])


def lane_codes(rows):
    total = rows[0:1, :]
    for s in range(1, 4):
        total = total + pltpu.roll(rows[s : s + 1, :], 16 * s, 1)
    return total + pltpu.roll(total, 64, 1)


def selection(codes, start, count, stride):
    place = lax.broadcasted_iota(jnp.int32, (count, 128), 0) + start
    half = lax.broadcasted_iota(jnp.int32, (count, 128), 1) >> 6
    picked = []
    for pair in range(2):
        wanted = (place + (half + 2 * pair) * stride).astype(F32)
        picked.append(jnp.where(codes == wanted, 1.0, 0.0).astype(BF16))
    return jnp.concatenate(picked, axis=1)


def edge_selection(codes):
    place = lax.broadcasted_iota(jnp.int32, (128, 128), 0)
    place = place + jnp.where(place >= 64, 384, 0)
    half = lax.broadcasted_iota(jnp.int32, (128, 128), 1) >> 6
    picked = []
    for pair in range(2):
        wanted = (place + (half + 2 * pair) * 512).astype(F32)
        picked.append(jnp.where(codes == wanted, 1.0, 0.0).T)
    return jnp.concatenate(picked, axis=0).astype(BF16)


def slot_rows(got, near, target, d):
    rows = []
    for c in range(3):
        for s in range(4):
            rows.append(got[s, c * PICK + near * 8 : c * PICK + near * 8 + 8, :])
            more = got[s, c * PICK + 24 : c * PICK + 32, :]
            rows.append(jnp.where(target == d.astype(F32), more, 0.0))
    return jnp.concatenate(rows, axis=0)


def contributions(rows, table_h, table_l):
    high, low = split(rows)
    product = dot(high, table_h) + dot(low, table_h) + dot(high, table_l)
    return split(
        jnp.concatenate(
            [
                jnp.concatenate(
                    [product[64 * c : 64 * c + 64, 128 * k : 128 * k + 128] for c in range(3)], axis=1
                )
                for k in range(4)
            ],
            axis=0,
        )
    )


def stacked(interp):
    return split(jnp.concatenate([interp[k] for k in range(4)], axis=1))


def neighbour(g, side):
    other = g - 1 if side == 0 else g + 1
    return (other >= 0) & (other < 4), jnp.clip(other, 0, 3)


def border(
    got, field, source, mass, interp, codes,
    pay1, pay2, rim, rim_diag, corner_diag, y_high, y_low, corners,
):
    g = lax.axis_index("group")
    odd = lax.axis_index("curve") & 1
    target = codes[16:24, :]
    table_h, table_l = stacked(interp)
    own = codes[8:9, :]
    high, low = contributions(slot_rows(got, 1, target, g), table_h, table_l)
    y_high[...] = high
    y_low[...] = low
    for end, start in ((0, 0), (64, 448)):
        chosen = selection(own, start, 64, 512)
        added = dot(chosen, high) + dot(chosen, low)
        rim_diag[end : end + 64, :] = OMEGA / (6.0 + mass[start : start + 64, :])
        for c in range(3):
            rim[c, end : end + 64, :] = field[c, start : start + 64, :] + added[:, c * 128 : c * 128 + 128]

    corner_diag[...] = jnp.zeros((8, 128), F32)
    line = lax.broadcasted_iota(jnp.int32, (8, 64), 0)
    wanted = ((line >> 1) * 32 + (line & 1) * 15).astype(F32)
    for side in range(2):
        exists, s = neighbour(g, side)
        theirs = lane_codes(got.at[s, A_CODE : A_CODE + 8, :])
        chosen = jnp.where(theirs[:, 0:64] == wanted, 1.0, 0.0).astype(BF16)
        rows = slot_rows(got, 2 * side, target, s)
        high, low = split(jnp.concatenate([rows[64 * c : 64 * c + 64] for c in range(3)], axis=1))
        merged = dot(chosen, high) + dot(chosen, low)
        high, low = split(jnp.concatenate([merged[:, 128 * c : 128 * c + 128] for c in range(3)], axis=0))
        product = dot(high, table_h) + dot(low, table_h) + dot(high, table_l)
        for end in range(2):
            x = 15 * end
            at = 2 * side + end
            corner_diag[at : at + 1, :] = jnp.where(exists, got[s, A_DIAG + x : A_DIAG + x + 1, :], 0.0)
            for c in range(3):
                value = got[s, A_EDGE + 16 * c + x : A_EDGE + 16 * c + x + 1, :]
                for k in range(4):
                    line_at = 8 * c + 2 * k + end
                    value = value + product[line_at : line_at + 1, 128 * k : 128 * k + 128]
                corners[end, 4 * side + c : 4 * side + c + 1, :] = jnp.where(exists, value, 0.0)

    for pay, upper in ((pay1, 1 - odd), (pay2, odd)):
        at = pl.multiple_of(upper * 96, 32)
        inner = pl.multiple_of(upper * 32 + 32, 32)
        whole = pl.multiple_of(upper * 480, 32)
        diag = rim_diag[pl.ds(at, 32), :]
        pay[B_DIAG : B_DIAG + 32, :] = diag
        pay[B_CORN : B_CORN + 8, :] = corners[upper]
        for c in range(3):
            first = rim[c, pl.ds(at, 32), :]
            left = corners[upper, c : c + 1, :]
            right = corners[upper, 4 + c : 5 + c, :]
            beside = rim[c, pl.ds(inner, 32), :] + row_pair(first, left, right) + z_pair(first)
            pay[32 * c : 32 * c + 32, :] = first
            pay[B_PART + 32 * c : B_PART + 32 * c + 32, :] = first * THIRD + diag * (
                source[c, pl.ds(whole, 32), :] + beside
            )


def goes_early():
    c = lax.axis_index("curve")
    return ((c % 64 == 0) & (c > 0)) | (c % 64 == 1)


def smooth(
    early, got, field, source, mass, interp, y_high, y_low, codes, children, kinds, pay,
    state, base, sel, table_h, table_l, passed, cst, mid, near, sweep, diag, child, kind, sems,
):
    passed[...] = pay[...]

    @pl.when(goes_early() == early)
    def _():
        copies = [
            pltpu.make_async_copy(children, child, sems.at[0]),
            pltpu.make_async_copy(kinds, kind, sems.at[1]),
        ]
        for copy in copies:
            copy.start()
        g = lax.axis_index("group")
        target = codes[16:24, :]
        for k in range(4):
            table_h[k], table_l[k] = split(interp[k])
        own = codes[8:9, :]
        sel[...] = edge_selection(own)
        for q in range(4):
            chosen = selection(own, q * 128, 128, 512)
            added = dot(chosen, y_high[...]) + dot(chosen, y_low[...])
            rows = slice(q * 128, q * 128 + 128)
            diag[rows, :] = OMEGA / (6.0 + mass[rows, :])
            for c in range(3):
                cst[c, rows, :] = field[c, rows, :] + added[:, c * 128 : c * 128 + 128]

        stack_h, stack_l = stacked(interp)
        for side in range(2):
            exists, s = neighbour(g, side)
            high, low = contributions(slot_rows(got, 2 * side, target, s), stack_h, stack_l)
            chosen = selection(lane_codes(got.at[s, A_CODE : A_CODE + 8, :]), 0, 32, 32)
            added = dot(chosen, high) + dot(chosen, low)
            beyond = got[s, A_DIAG : A_DIAG + 16, :]
            for c in range(3):
                first = added[0:16, c * 128 : c * 128 + 128]
                second = added[16:32, c * 128 : c * 128 + 128]
                edge = got[s, A_EDGE + 16 * c : A_EDGE + 16 * c + 16, :] + first
                near[side, c] = jnp.where(exists, edge, 0.0)
                beside = second + row_pair(first, 0.0, 0.0) + z_pair(first)
                beside = beside + column(cst, c, 0 if side == 0 else 31)
                part = got[s, A_PART + 16 * c : A_PART + 16 * c + 16, :] + first * THIRD
                sweep[side, c] = jnp.where(exists, part + beyond * beside, 0.0)

        def step(before, halo, result):
            for x in range(16):
                rows = slice(32 * x, 32 * x + 32)
                d = diag[rows, :]
                for c in range(3):
                    centre = before[c, rows, :]
                    beside = row_pair(centre, halo[0, c, x : x + 1, :], halo[1, c, x : x + 1, :]) + z_pair(centre)
                    if x > 0:
                        beside = beside + before[c, 32 * x - 32 : 32 * x, :]
                    if x < 15:
                        beside = beside + before[c, 32 * x + 32 : 32 * x + 64, :]
                    result[c, rows, :] = centre * THIRD + d * (source[c, rows, :] + beside)

        step(cst, near, mid)
        step(mid, sweep, state)
        base[...] = jnp.zeros(base.shape, F32)
        for copy in copies:
            copy.wait()
        for s in range(4):
            for k in range(16):
                b = child[0, 0, s, k]
                row = kind[0, 0, s, k] * 64 + (s * 16 + k)
                for c in range(3):
                    base[c, pl.ds(row, 1), :] = state[c, pl.ds(b, 1), :] - cst[c, pl.ds(b, 1), :]


def restrict(rim, rim_diag, corner_diag, got1, got2, *rest):
    early_set, late_set, (fix, out) = rest[:4], rest[4:8], rest[8:]
    odd = lax.axis_index("curve") & 1
    for got, upper in ((got1, 1 - odd), (got2, odd)):
        at = pl.multiple_of(upper * 96, 32)
        inner = pl.multiple_of(upper * 32 + 32, 32)
        d_edge = rim_diag[pl.ds(at, 32), :]
        d_inner = rim_diag[pl.ds(inner, 32), :]
        far = got[B_DIAG : B_DIAG + 32, :]
        for c in range(3):
            beyond = got[B_PART + 32 * c : B_PART + 32 * c + 32, :] + far * rim[c, pl.ds(at, 32), :]
            first = d_edge * got[32 * c : 32 * c + 32, :]
            left = corner_diag[pl.ds(upper, 1), :] * got[B_CORN + c : B_CORN + c + 1, :]
            right = corner_diag[pl.ds(2 + upper, 1), :] * got[B_CORN + 4 + c : B_CORN + 5 + c, :]
            beside = beyond + row_pair(first, left, right) + z_pair(first)
            fix[c, pl.ds(at, 32), :] = first * THIRD + d_edge * beside
            fix[c, pl.ds(inner, 32), :] = d_inner * first
    high, low = split(jnp.concatenate([fix[c] for c in range(3)], axis=1))

    def finish(base, sel, table_h, table_l):
        rows = dot(sel[...], high) + dot(sel[...], low)
        total = None
        for k in range(4):
            at = slice(64 * k, 64 * k + 64)
            placed = [base[c, at, :] + rows[at, 128 * c : 128 * c + 128] for c in range(3)]
            p_high, p_low = split(jnp.concatenate(placed, axis=0))
            product = dot_t(p_high, table_h[k]) + dot_t(p_low, table_h[k]) + dot_t(p_high, table_l[k])
            total = product if total is None else total + product
        for s in range(4):
            for c in range(3):
                out[s, 16 * c : 16 * c + 16, :] = total[64 * c + 16 * s : 64 * c + 16 * s + 16, :]

    early = goes_early()

    @pl.when(early)
    def _():
        finish(*early_set)

    @pl.when(jnp.logical_not(early))
    def _():
        finish(*late_set)


def collect(early_state, late_state, fix, got, codes, out, result, sems):
    total = codes[0:1, :]
    rows = jnp.concatenate(
        [
            jnp.concatenate([got[d, 16 * c : 16 * c + 16, :] for d in range(4)], axis=0)
            for c in range(3)
        ],
        axis=1,
    )
    high, low = split(rows)
    place = lax.broadcasted_iota(jnp.int32, (128, 64), 0)

    def finish(state):
        copies = []
        for q in range(4):
            picked = jnp.where(total[:, 0:64] == (place + q * 128).astype(F32), 1.0, 0.0).astype(BF16)
            added = dot(picked, high) + dot(picked, low)
            for c in range(3):
                at = slice(q * 128, q * 128 + 128)
                final = state[c, at, :] + added[:, c * 128 : c * 128 + 128]
                if q == 0:
                    final = jnp.concatenate([final[0:64] + fix[c, 0:64, :], final[64:128]], axis=0)
                if q == 3:
                    final = jnp.concatenate([final[0:64], final[64:128] + fix[c, 64:128, :]], axis=0)
                result[c, at, :] = final
                copy = pltpu.make_async_copy(result.at[c, at, :], out.at[c, at, :], sems.at[len(copies)])
                copy.start()
                copies.append(copy)
        for copy in copies:
            copy.wait()

    early = goes_early()

    @pl.when(early)
    def _():
        finish(early_state)

    @pl.when(jnp.logical_not(early))
    def _():
        finish(late_state)


def stay(array):
    return pltpu.with_memory_space_constraint(array, pltpu.HBM)


def shape(*dims, kind=F32):
    return jax.ShapeDtypeStruct(dims, kind)


def call(body, outs, ins, scratch=(), aliases=None, to=VMEM, flops=1_000_000, moved=1_000_000, limit=16384):
    many = isinstance(outs, list)
    return pl.pallas_call(
        body,
        out_shape=outs,
        in_specs=ins,
        out_specs=[to] * len(outs) if many else to,
        scratch_shapes=list(scratch),
        input_output_aliases=aliases or {},
        cost_estimate=pl.CostEstimate(flops=flops, bytes_accessed=moved, transcendentals=0),
        compiler_params=pltpu.CompilerParams(vmem_limit_bytes=limit << 10),
    )


def local(field, source, mass, interp, parents, children, kinds, counts):
    whole = field.shape
    send, codes, field = call(
        pack,
        [shape(4, A_ROWS, 128), shape(24, 128), shape(3, 512, 128)],
        [HBM] * 7,
        [
            pltpu.VMEM((2, 3, 16, 8, 128), F32),
            pltpu.VMEM((2, 16, 8, 128), F32),
            pltpu.SMEM(parents.shape, jnp.int32),
            pltpu.SMEM(counts.shape, jnp.int32),
            pltpu.VMEM(parents.shape, jnp.int32),
            pltpu.VMEM(parents.shape, jnp.int32),
            pltpu.VMEM(parents.shape, jnp.int32),
            pltpu.VMEM((120, 128), F32),
            pltpu.SemaphoreType.DMA((12,)),
        ],
    )(*map(stay, (field.reshape(3, 512, 128), source, mass, parents, counts, children, kinds)))
    source = source.reshape(3, 512, 128)
    mass = mass.reshape(512, 128)
    got = lax.all_to_all(send, "group", 0, 0, tiled=True)
    pay1, pay2, rim, rim_diag, corner_diag, y_high, y_low = call(
        border,
        [
            shape(B_ROWS, 128),
            shape(B_ROWS, 128),
            shape(3, 128, 128),
            shape(128, 128),
            shape(8, 128),
            shape(256, 384, kind=BF16),
            shape(256, 384, kind=BF16),
        ],
        [VMEM] * 6,
        [pltpu.VMEM((2, 8, 128), F32)],
    )(got, field, source, mass, interp, codes)

    def smoothed(early, pay):
        return call(
            functools.partial(smooth, early),
            [
                shape(3, 512, 128),
                shape(3, 256, 128),
                shape(256, 128, kind=BF16),
                shape(4, 128, 128, kind=BF16),
                shape(4, 128, 128, kind=BF16),
                shape(*pay.shape),
            ],
            [VMEM] * 8 + [HBM] * 2 + [VMEM],
            [
                pltpu.VMEM((3, 512, 128), F32),
                pltpu.VMEM((3, 512, 128), F32),
                pltpu.VMEM((2, 3, 16, 128), F32),
                pltpu.VMEM((2, 3, 16, 128), F32),
                pltpu.VMEM((512, 128), F32),
                pltpu.SMEM(children.shape, jnp.int32),
                pltpu.SMEM(kinds.shape, jnp.int32),
                pltpu.SemaphoreType.DMA((2,)),
            ],
            flops=20_000_000,
            moved=8_000_000,
        )(got, field, source, mass, interp, y_high, y_low, codes, stay(children), stay(kinds), pay)

    *early_set, pay2 = smoothed(True, pay2)
    count = lax.axis_size("curve")
    inner = [(i, i ^ 1) for i in range(count)]
    outer = [(i, i + 1) for i in range(1, count - 1, 2)]
    outer = outer + [(b, a) for a, b in outer]
    got2 = lax.ppermute(pay2, "curve", outer)
    got1 = lax.ppermute(pay1, "curve", inner)
    *late_set, _ = smoothed(False, corner_diag)
    fix, send = call(
        restrict, [shape(3, 128, 128), shape(4, 48, 128)], [VMEM] * 13
    )(rim, rim_diag, corner_diag, got1, got2, *early_set[1:], *late_set[1:])
    got = lax.all_to_all(send, "group", 0, 0, tiled=True)
    out = call(
        collect,
        shape(3, 512, 128),
        [VMEM] * 5,
        [pltpu.VMEM((3, 512, 128), F32), pltpu.SemaphoreType.DMA((12,))],
        to=HBM,
    )(early_set[0], late_set[0], fix, got, codes)
    return out.reshape(whole)


def solution(mesh):
    in_specs = (
        P(None, "curve", "group", None),
        P(None, "curve", "group", None),
        P("curve", "group", None),
        P(),
        P("curve", "group", None, None),
        P("curve", "group", None, None),
        P("curve", "group", None, None),
        P("curve", "group", None),
    )
    out_specs = P(None, "curve", "group", None)
    return jax.shard_map(local, mesh=mesh, in_specs=in_specs, out_specs=out_specs, check_vma=False)
```

time: 51.8 us -> 49.6 us (0.958)
  starting transfers between devices: 21 us -> 18.8 us
  waiting for transfers between devices: 0.63 us -> 1.85 us
  local copies, waits for them, and re-layouts: 0.69 us -> 0.01 us
  Pallas kernels: 8 us -> 7.41 us
    ppermute x1, starting transfers between devices: 19.1 us -> 16.9 us  [local(): got2 = lax.ppermute(pay2, 'curve', outer)]
    ppermute x1, waiting for transfers between devices: 0.63 us -> 1.85 us  [local(): got2 = lax.ppermute(pay2, 'curve', outer)]
    unnamed x12 -> x6, local copies, waits for them, and re-layouts: 0.69 us -> 0.01 us
    pallas_call x5 -> x6, Pallas kernels: 8 us -> 7.41 us  [the longest x2 2.81 us: smoothed(): call(functools.partial(smooth, early), [shape(3, 512, 128), shape(3, 256,...]
  transfers between devices with their start and end apart: 2 -> 2, of which waited for: 1 -> 1; matrix products, arithmetic and copies ran while one was open for 0% -> 0% of each run, Pallas kernels for 4% -> 6%
where the time goes in v3:
time: 49.6 us; the launch traced here: 49.4 us
  blocking collectives  21.2 us (43%)
  starting transfers between devices  18.8 us (38%)
  Pallas kernels  7.41 us (15%)
  waiting for transfers between devices  1.85 us (4%)
    all_to_all x2, blocking collectives, local(): got = lax.all_to_all(send, 'group', 0, 0, tiled=True)  21.2 us
    ppermute x1, starting transfers between devices, local(): got2 = lax.ppermute(pay2, 'curve', outer)  16.9 us
    pallas_call x2, Pallas kernels, smoothed(): call(functools.partial(smooth, early), [shape(3, 512, 128), shape(3, 256,...  2.81 us
    ppermute x1, starting transfers between devices, local(): got1 = lax.ppermute(pay1, 'curve', inner)  1.92 us
    ppermute x1, waiting for transfers between devices, local(): got2 = lax.ppermute(pay2, 'curve', outer)  1.85 us
    pallas_call x1, Pallas kernels, local(): call(pack, [shape(4, A_ROWS, 128), shape(24, 128), shape(3, 512, 128)], [...  1.61 us
    pallas_call x1, Pallas kernels, local(): call(collect, shape(3, 512, 128), [VMEM] * 5, [pltpu.VMEM((3, 512, 128),...  1.19 us
    pallas_call x1, Pallas kernels, local(): call(border, [shape(B_ROWS, 128), shape(B_ROWS, 128), shape(3, 128, 128),...  1.01 us
  transfers between devices with their start and end apart: 2, of which 1 were waited for; matrix products, arithmetic and copies ran while one was open for 0% of the time, Pallas kernels for 6%

profile of v3, /device:TPU:6, one launch (start us, length us, event | category | flops | bytes accessed | tf_op | source)
XLA Modules:
  0.0 49.4 jit_solution(3838913181323495954)
XLA Ops:
  0.0 0.0 copy-start.1
  0.0 0.0 copy-start.2
  0.0 1.6 %shard_map.82 = (f32[4,216,128]{2,1,0:T(8,128)S(1)}, f32[24,128]{1,0:T(8,128)S(1)}, f32[3,512,128]{2,1,0:T(8,128)S(1)}) custom-call(f32[3,512,128]{2,1,0:T(8,128)} %bitcast.10, f32[3,16,32,128]{3,2,1,0:T(8,128)} %source.1, f32[16,32,128]{2,1,0:T(8,128)} %mass.1, s32[1,1,4,16]{3,2,1,0:T(4,128)} %parents.1, s32[1,1,4]{2,1,0:T(1,128)} %counts.1, ...), custom_call_target="tpu_custom_call" | custom-call | flops 1000000 | bytes 1000000 | tf_op jit(solution)/shard_map/pallas_call | solution.py:457
  1.6 0.0 copy-start
  1.6 13.0 %all_to_all.10.got = f32[4,216,128]{2,1,0:T(8,128)S(1)} all-to-all(f32[4,216,128]{2,1,0:T(8,128)S(1)} %get-tuple-element.28), channel_id=1, replica_groups=mesh['curve'=256,'group'=4] {'group'}, dimensions={0} | all-to-all | bytes 884736 | tf_op jit(solution)/shard_map/all_to_all | solution.py:475
  14.6 0.0 copy-done.1
  14.6 0.0 copy-done.2
  14.6 0.0 copy-done
  14.6 1.0 %shard_map.83 = (f32[232,128]{1,0:T(8,128)S(1)}, f32[232,128]{1,0:T(8,128)S(1)}, f32[3,128,128]{2,1,0:T(8,128)S(1)}, f32[128,128]{1,0:T(8,128)S(1)}, f32[8,128]{...) custom-call(f32[4,216,128]{2,1,0:T(8,128)S(1)} %all_to_all.10.got, ...), custom_call_target="tpu_custom_call" | custom-call | flops 1000000 | bytes 1000000 | tf_op jit(solution)/shard_map/pallas_call | solution.py:476
  15.7 1.9 %collective-permute-start = (f32[232,128]{1,0:T(8,128)S(1)}, f32[232,128]{1,0:T(8,128)S(1)}, u32[]{:S(2)}, u32[]{:S(2)}) collective-permute-start(f32[232,128]{1,0:T(8,128)S(1)} %get-tuple-element.39), channel_id=1, source_target_pairs={{0,4},{4,0},{8,12},{12,8},{16,20},{20,16},{24,28},{28,24},{32,36},... | collective-permute-start | bytes 356360 | tf_op jit(solution)/shard_map/ppermute | solution.py:523
  17.6 2.2 %shard_map.84 = (f32[3,512,128]{2,1,0:T(8,128)S(1)}, f32[3,256,128]{2,1,0:T(8,128)S(1)}, bf16[256,128]{1,0:T(8,128)(2,1)S(1)}, bf16[4,128,128]{2,1,0:T(8,128)(2,...) custom-call(f32[4,216,128]{2,1,0:T(8,128)S(1)} %all_to_all.10.got, ...), custom_call_target="tpu_custom_call" | custom-call | flops 20000000 | bytes 8000000 | tf_op jit(solution)/shard_map/pallas_call | solution.py:492
  19.8 16.9 %collective-permute-start.1 = (f32[232,128]{1,0:T(8,128)S(1)}, f32[232,128]{1,0:T(8,128)S(1)}, u32[]{:S(2)}, u32[]{:S(2)}) collective-permute-start(f32[232,128]{1,0:T(8,128)S(1)} %get-tuple-element.40), channel_id=1, source_target_pairs={{4,8},{12,16},{20,24},{28,32},{36,40},{44,48},{52,56},{60,64},{68,... | collective-permute-start | bytes 356360 | tf_op jit(solution)/shard_map/ppermute | solution.py:522
  36.7 0.6 %shard_map.85 = (f32[3,512,128]{2,1,0:T(8,128)S(1)}, f32[3,256,128]{2,1,0:T(8,128)S(1)}, bf16[256,128]{1,0:T(8,128)(2,1)S(1)}, bf16[4,128,128]{2,1,0:T(8,128)(2,...) custom-call(f32[4,216,128]{2,1,0:T(8,128)S(1)} %all_to_all.10.got, ...), custom_call_target="tpu_custom_call" | custom-call | flops 20000000 | bytes 8000000 | tf_op jit(solution)/shard_map/pallas_call | solution.py:492
  37.3 0.0 collective-permute-done.got1
  37.3 1.9 %collective-permute-done.1.got2 = f32[232,128]{1,0:T(8,128)S(1)} collective-permute-done((f32[232,128]{1,0:T(8,128)S(1)}, f32[232,128]{1,0:T(8,128)S(1)}, u32[]{:S(2)}, u32[]{:S(2)}) %collective-permute-start.1) | collective-permute-done | bytes 118816 | tf_op jit(solution)/shard_map/ppermute | solution.py:522
  39.2 0.8 %shard_map.86 = (f32[3,128,128]{2,1,0:T(8,128)S(1)}, f32[4,48,128]{2,1,0:T(8,128)S(1)}) custom-call(f32[3,128,128]{2,1,0:T(8,128)S(1)} %get-tuple-element.37.rim, f32[128,128]{1,0:T(8,128)S(1)} %get-tuple-element.38.rim_diag, f32[8,128]{1,0:T(8,128)S(1)} %get-tuple-element.35.pay.corner_diag, f32[232,128]{1,0:T(8,128)S(1)} %collective-permute-done.got1, ...), custom_call_target="tpu_custom_call" | custom-call | flops 1000000 | bytes 1000000 | tf_op jit(solution)/shard_map/pallas_call | solution.py:525
  40.0 8.2 %all_to_all.11.got = f32[4,48,128]{2,1,0:T(8,128)S(1)} all-to-all(f32[4,48,128]{2,1,0:T(8,128)S(1)} %get-tuple-element.50), channel_id=1, replica_groups=mesh['curve'=256,'group'=4] {'group'}, dimensions={0} | all-to-all | bytes 196608 | tf_op jit(solution)/shard_map/all_to_all | solution.py:528
  48.2 1.2 %shard_map.87 = f32[3,512,128]{2,1,0:T(8,128)} custom-call(f32[3,512,128]{2,1,0:T(8,128)S(1)} %get-tuple-element.34.early_state, f32[3,512,128]{2,1,0:T(8,128)S(1)} %get-tuple-element.36.late_state, f32[3,128,128]{2,1,0:T(8,128)S(1)} %get-tuple-element.49.fix, f32[4,48,128]{2,1,0:T(8,128)S(1)} %all_to_all.11.got, f32[24,128]{1,0:T(8,128)S(1)} %get-tuple-element.30.codes), custom_call_target="tpu_custom_call" | custom-call | flops 1000000 | bytes 1000000 | tf_op jit(solution)/shard_map/pallas_call | solution.py:529
Async XLA Ops:
  0.0 14.6 %copy-start.1 = (f32[16,32,128]{2,1,0:T(8,128)S(1)}, f32[16,32,128]{2,1,0:T(8,128)}, u32[]{:S(2)}) copy-start(f32[16,32,128]{2,1,0:T(8,128)} %mass.1) | copy-start | bytes 786436
  0.0 14.6 %copy-start.2 = (f32[4,128,128]{2,1,0:T(8,128)S(1)}, f32[4,128,128]{2,1,0:T(8,128)}, u32[]{:S(2)}) copy-start(f32[4,128,128]{2,1,0:T(8,128)} %interp.5) | copy-start | bytes 786436
  1.6 13.0 %copy-start = (f32[3,16,32,128]{3,2,1,0:T(8,128)S(1)}, f32[3,16,32,128]{3,2,1,0:T(8,128)}, u32[]{:S(2)}) copy-start(f32[3,16,32,128]{3,2,1,0:T(8,128)} %source.1) | copy-start | bytes 2359300
  15.7 21.7 %collective-permute-start = (f32[232,128]{1,0:T(8,128)S(1)}, f32[232,128]{1,0:T(8,128)S(1)}, u32[]{:S(2)}, u32[]{:S(2)}) collective-permute-start(f32[232,128]{1,0:T(8,128)S(1)} %get-tuple-element.39), channel_id=1, source_target_pairs={{0,4},{4,0},{8,12},{12,8},{16,20},{20,16},{24,28},{28,24},{32,36},... | collective-permute-start | bytes 356360 | tf_op jit(solution)/shard_map/ppermute | solution.py:523
  19.8 19.4 %collective-permute-start.1 = (f32[232,128]{1,0:T(8,128)S(1)}, f32[232,128]{1,0:T(8,128)S(1)}, u32[]{:S(2)}, u32[]{:S(2)}) collective-permute-start(f32[232,128]{1,0:T(8,128)S(1)} %get-tuple-element.40), channel_id=1, source_target_pairs={{4,8},{12,16},{20,24},{28,32},{36,40},{44,48},{52,56},{60,64},{68,... | collective-permute-start | bytes 356360 | tf_op jit(solution)/shard_map/ppermute | solution.py:522

commit v4 on v3

--- a/solution.py
+++ b/solution.py
@@ -69,8 +69,8 @@
 
 
 def pack(
-    field, source, mass, parents, counts, children, kinds, out, codes, f_all,
-    s_edge, m_edge, p_scalar, c_scalar, p_lane, child, kind, rows, sems,
+    field, source, mass, parents, counts, children, kinds, out, codes, f_all, m_all,
+    s_edge, p_scalar, c_scalar, p_lane, child, kind, rows, sems,
 ):
     copies = [
         pltpu.make_async_copy(parents, p_scalar, sems.at[0]),
@@ -81,10 +81,9 @@
         pltpu.make_async_copy(children, child, sems.at[5]),
         pltpu.make_async_copy(kinds, kind, sems.at[6]),
         pltpu.make_async_copy(parents, p_lane, sems.at[7]),
-        pltpu.make_async_copy(source.at[:, :, 0:8, :], s_edge.at[0], sems.at[8]),
-        pltpu.make_async_copy(source.at[:, :, 24:32, :], s_edge.at[1], sems.at[9]),
-        pltpu.make_async_copy(mass.at[:, 0:8, :], m_edge.at[0], sems.at[10]),
-        pltpu.make_async_copy(mass.at[:, 24:32, :], m_edge.at[1], sems.at[11]),
+        pltpu.make_async_copy(source.at[:, :, 0, :], s_edge.at[0], sems.at[8]),
+        pltpu.make_async_copy(source.at[:, :, 31, :], s_edge.at[1], sems.at[9]),
+        pltpu.make_async_copy(mass, m_all, sems.at[10]),
     ]
     for copy in copies:
         copy.start()
@@ -125,13 +124,13 @@
     x = block >> 5
     sides = []
     for side, edge, inner, depth in ((0, 0, 1, y), (1, 31, 30, 31 - y)):
-        diag = OMEGA / (6.0 + m_edge[side, :, 7 * side, :])
+        diag = OMEGA / (6.0 + m_all[pl.ds(edge, 16, stride=32), :])
         firsts, parts = [], []
         for c in range(3):
             first = column(f_all, c, edge)
             beside = column(f_all, c, inner) + row_pair(first, 0.0, 0.0) + z_pair(first)
             firsts.append(first)
-            parts.append(first * THIRD + diag * (s_edge[side, c, :, 7 * side, :] + beside))
+            parts.append(first * THIRD + diag * (s_edge[side, c] + beside))
         code = jnp.where(depth < 2, kind[0, 0] * 32 + depth * 16 + x, -1)
         sides.append((firsts, parts, diag, code.astype(F32)))
     for p in range(4):
@@ -269,16 +268,23 @@
             )
 
 
+def waits():
+    c = lax.axis_index("curve")
+    return (c >= 64) & (c % 64 < 2)
+
+
 def goes_early():
     c = lax.axis_index("curve")
     return ((c % 64 == 0) & (c > 0)) | (c % 64 == 1)
 
 
-def smooth(
-    early, got, field, source, mass, interp, y_high, y_low, codes, children, kinds, pay,
-    state, base, sel, table_h, table_l, passed, cst, mid, near, sweep, diag, child, kind, sems,
-):
-    passed[...] = pay[...]
+def smooth(early, got, field, source, mass, interp, y_high, y_low, codes, children, kinds, *rest):
+    if early:
+        pay, *rest = rest
+        state, base, sel, table_h, table_l, passed, cst, mid, near, sweep, diag, child, kind, sems = rest
+        passed[...] = pay[...]
+    else:
+        state, base, sel, table_h, table_l, cst, mid, near, sweep, diag, child, kind, sems = rest
 
     @pl.when(goes_early() == early)
     def _():
@@ -345,10 +351,11 @@
                     base[c, pl.ds(row, 1), :] = state[c, pl.ds(b, 1), :] - cst[c, pl.ds(b, 1), :]
 
 
-def restrict(rim, rim_diag, corner_diag, got1, got2, *rest):
+def restrict(rim, rim_diag, corner_diag, got_first, got_last, got2, *rest):
     early_set, late_set, (fix, out) = rest[:4], rest[4:8], rest[8:]
     odd = lax.axis_index("curve") & 1
-    for got, upper in ((got1, 1 - odd), (got2, odd)):
+    got1 = jnp.where(waits(), got_first[...], got_last[...])
+    for got, upper in ((got1, 1 - odd), (got2[...], odd)):
         at = pl.multiple_of(upper * 96, 32)
         inner = pl.multiple_of(upper * 32 + 32, 32)
         d_edge = rim_diag[pl.ds(at, 32), :]
@@ -454,24 +461,22 @@
 
 def local(field, source, mass, interp, parents, children, kinds, counts):
     whole = field.shape
-    send, codes, field = call(
+    send, codes, field, mass = call(
         pack,
-        [shape(4, A_ROWS, 128), shape(24, 128), shape(3, 512, 128)],
+        [shape(4, A_ROWS, 128), shape(24, 128), shape(3, 512, 128), shape(512, 128)],
         [HBM] * 7,
         [
-            pltpu.VMEM((2, 3, 16, 8, 128), F32),
-            pltpu.VMEM((2, 16, 8, 128), F32),
+            pltpu.VMEM((2, 3, 16, 128), F32),
             pltpu.SMEM(parents.shape, jnp.int32),
             pltpu.SMEM(counts.shape, jnp.int32),
             pltpu.VMEM(parents.shape, jnp.int32),
             pltpu.VMEM(parents.shape, jnp.int32),
             pltpu.VMEM(parents.shape, jnp.int32),
             pltpu.VMEM((120, 128), F32),
-            pltpu.SemaphoreType.DMA((12,)),
+            pltpu.SemaphoreType.DMA((11,)),
         ],
-    )(*map(stay, (field.reshape(3, 512, 128), source, mass, parents, counts, children, kinds)))
+    )(*map(stay, (field.reshape(3, 512, 128), source, mass.reshape(512, 128), parents, counts, children, kinds)))
     source = source.reshape(3, 512, 128)
-    mass = mass.reshape(512, 128)
     got = lax.all_to_all(send, "group", 0, 0, tiled=True)
     pay1, pay2, rim, rim_diag, corner_diag, y_high, y_low = call(
         border,
@@ -488,7 +493,7 @@
         [pltpu.VMEM((2, 8, 128), F32)],
     )(got, field, source, mass, interp, codes)
 
-    def smoothed(early, pay):
+    def smoothed(early, *pay):
         return call(
             functools.partial(smooth, early),
             [
@@ -497,9 +502,9 @@
                 shape(256, 128, kind=BF16),
                 shape(4, 128, 128, kind=BF16),
                 shape(4, 128, 128, kind=BF16),
-                shape(*pay.shape),
+                *(shape(*p.shape) for p in pay),
             ],
-            [VMEM] * 8 + [HBM] * 2 + [VMEM],
+            [VMEM] * 8 + [HBM] * 2 + [VMEM] * len(pay),
             [
                 pltpu.VMEM((3, 512, 128), F32),
                 pltpu.VMEM((3, 512, 128), F32),
@@ -512,19 +517,22 @@
             ],
             flops=20_000_000,
             moved=8_000_000,
-        )(got, field, source, mass, interp, y_high, y_low, codes, stay(children), stay(kinds), pay)
+        )(got, field, source, mass, interp, y_high, y_low, codes, stay(children), stay(kinds), *pay)
 
     *early_set, pay2 = smoothed(True, pay2)
     count = lax.axis_size("curve")
-    inner = [(i, i ^ 1) for i in range(count)]
+    waiting = [i for i in range(64, count) if i % 64 < 2]
+    inner_first = [(i, i ^ 1) for i in waiting]
+    inner_last = [(i, i ^ 1) for i in range(count) if i not in waiting]
     outer = [(i, i + 1) for i in range(1, count - 1, 2)]
     outer = outer + [(b, a) for a, b in outer]
+    got_first = lax.ppermute(pay1, "curve", inner_first)
     got2 = lax.ppermute(pay2, "curve", outer)
-    got1 = lax.ppermute(pay1, "curve", inner)
-    *late_set, _ = smoothed(False, corner_diag)
+    got_last = lax.ppermute(pay1, "curve", inner_last)
+    late_set = smoothed(False)
     fix, send = call(
-        restrict, [shape(3, 128, 128), shape(4, 48, 128)], [VMEM] * 13
-    )(rim, rim_diag, corner_diag, got1, got2, *early_set[1:], *late_set[1:])
+        restrict, [shape(3, 128, 128), shape(4, 48, 128)], [VMEM] * 14
+    )(rim, rim_diag, corner_diag, got_first, got_last, got2, *early_set[1:], *late_set[1:])
     got = lax.all_to_all(send, "group", 0, 0, tiled=True)
     out = call(
         collect,

time: 49.6 us -> 50.2 us (1.012)
  starting transfers between devices: 18.8 us -> 19.5 us
  Pallas kernels: 7.41 us -> 6.73 us
  waiting for transfers between devices: 1.85 us -> 2.44 us
    ppermute x1 -> x2, starting transfers between devices: 1.92 us -> 2.59 us  [the longest x1 1.92 us: local(): got_first = lax.ppermute(pay1, 'curve', inner_first)]
    pallas_call x2, Pallas kernels: 2.81 us -> 2.22 us  [smoothed(): call(functools.partial(smooth, early), [shape(3, 512, 128), shape(3, 256,...]
    ppermute x1, waiting for transfers between devices: 1.85 us -> 2.43 us  [local(): got2 = lax.ppermute(pay2, 'curve', outer)]
  transfers between devices with their start and end apart: 2 -> 3, of which waited for: 1 -> 1; matrix products, arithmetic and copies ran while one was open for 0% -> 0% of each run, Pallas kernels for 6% -> 4%
where the time goes in v4:
time: 50.2 us; the launch traced here: 49.9 us
  blocking collectives  21.2 us (42%)
  starting transfers between devices  19.5 us (39%)
  Pallas kernels  6.73 us (13%)
  waiting for transfers between devices  2.44 us (5%)
    all_to_all x2, blocking collectives, local(): got = lax.all_to_all(send, 'group', 0, 0, tiled=True)  21.2 us
    ppermute x1, starting transfers between devices, local(): got2 = lax.ppermute(pay2, 'curve', outer)  16.9 us
    ppermute x1, waiting for transfers between devices, local(): got2 = lax.ppermute(pay2, 'curve', outer)  2.43 us
    pallas_call x2, Pallas kernels, smoothed(): call(functools.partial(smooth, early), [shape(3, 512, 128), shape(3, 256,...  2.22 us
    ppermute x1, starting transfers between devices, local(): got_first = lax.ppermute(pay1, 'curve', inner_first)  1.92 us
    pallas_call x1, Pallas kernels, local(): call(pack, [shape(4, A_ROWS, 128), shape(24, 128), shape(3, 512, 128), sh...  1.52 us
    pallas_call x1, Pallas kernels, local(): call(collect, shape(3, 512, 128), [VMEM] * 5, [pltpu.VMEM((3, 512, 128),...  1.18 us
  transfers between devices with their start and end apart: 3, of which 1 were waited for; matrix products, arithmetic and copies ran while one was open for 0% of the time, Pallas kernels for 4%

profile of v4, /device:TPU:6, one launch (start us, length us, event | category | flops | bytes accessed | tf_op | source)
XLA Modules:
  0.0 49.9 jit_solution(10908818467794319341)
XLA Ops:
  0.0 0.0 copy-start.1
  0.0 1.5 %shard_map.82 = (f32[4,216,128]{2,1,0:T(8,128)S(1)}, f32[24,128]{1,0:T(8,128)S(1)}, f32[3,512,128]{2,1,0:T(8,128)S(1)}, f32[512,128]{1,0:T(8,128)S(1)}) custom-call(f32[3,512,128]{2,1,0:T(8,128)} %bitcast.7, f32[3,16,32,128]{3,2,1,0:T(8,128)} %source.1, f32[512,128]{1,0:T(8,128)} %bitcast.8, s32[1,1,4,16]{3,2,1,0:T(4,128)} %parents.1, s32[1,1,4]{2,1,0:T(1,128)} %counts.1, ...), custom_call_target="tpu_custom_call" | custom-call | flops 1000000 | bytes 1000000 | tf_op jit(solution)/shard_map/pallas_call | solution.py:464
  1.5 0.0 copy-start
  1.5 13.0 %all_to_all.10.got = f32[4,216,128]{2,1,0:T(8,128)S(1)} all-to-all(f32[4,216,128]{2,1,0:T(8,128)S(1)} %get-tuple-element.29), channel_id=1, replica_groups=mesh['curve'=256,'group'=4] {'group'}, dimensions={0} | all-to-all | bytes 884736 | tf_op jit(solution)/shard_map/all_to_all | solution.py:480
  14.5 0.0 copy-done.1
  14.5 0.0 copy-done
  14.5 1.0 %shard_map.83 = (f32[232,128]{1,0:T(8,128)S(1)}, f32[232,128]{1,0:T(8,128)S(1)}, f32[3,128,128]{2,1,0:T(8,128)S(1)}, f32[128,128]{1,0:T(8,128)S(1)}, f32[8,128]{...) custom-call(f32[4,216,128]{2,1,0:T(8,128)S(1)} %all_to_all.10.got, ...), custom_call_target="tpu_custom_call" | custom-call | flops 1000000 | bytes 1000000 | tf_op jit(solution)/shard_map/pallas_call | solution.py:481
  15.6 1.9 %collective-permute-start = (f32[232,128]{1,0:T(8,128)S(1)}, f32[232,128]{1,0:T(8,128)S(1)}, u32[]{:S(2)}, u32[]{:S(2)}) collective-permute-start(f32[232,128]{1,0:T(8,128)S(1)} %get-tuple-element.41), channel_id=1, source_target_pairs={{256,260},{260,256},{512,516},{516,512},{768,772},{772,768},{257,2... | collective-permute-start | bytes 356360 | tf_op jit(solution)/shard_map/ppermute | solution.py:529
  17.5 0.7 %collective-permute-start.1 = (f32[232,128]{1,0:T(8,128)S(1)}, f32[232,128]{1,0:T(8,128)S(1)}, u32[]{:S(2)}, u32[]{:S(2)}) collective-permute-start(f32[232,128]{1,0:T(8,128)S(1)} %get-tuple-element.41), channel_id=1, source_target_pairs={{0,4},{4,0},{8,12},{12,8},{16,20},{20,16},{24,28},{28,24},{32,36},... | collective-permute-start | bytes 356360 | tf_op jit(solution)/shard_map/ppermute | solution.py:531
  18.2 2.2 %shard_map.84 = (f32[3,512,128]{2,1,0:T(8,128)S(1)}, f32[3,256,128]{2,1,0:T(8,128)S(1)}, bf16[256,128]{1,0:T(8,128)(2,1)S(1)}, bf16[4,128,128]{2,1,0:T(8,128)(2,...) custom-call(f32[4,216,128]{2,1,0:T(8,128)S(1)} %all_to_all.10.got, ...), custom_call_target="tpu_custom_call" | custom-call | flops 20000000 | bytes 8000000 | tf_op jit(solution)/shard_map/pallas_call | solution.py:497
  20.3 16.9 %collective-permute-start.2 = (f32[232,128]{1,0:T(8,128)S(1)}, f32[232,128]{1,0:T(8,128)S(1)}, u32[]{:S(2)}, u32[]{:S(2)}) collective-permute-start(f32[232,128]{1,0:T(8,128)S(1)} %get-tuple-element.42), channel_id=1, source_target_pairs={{4,8},{12,16},{20,24},{28,32},{36,40},{44,48},{52,56},{60,64},{68,... | collective-permute-start | bytes 356360 | tf_op jit(solution)/shard_map/ppermute | solution.py:530
  37.3 0.0 collective-permute-done.got_first
  37.3 0.0 collective-permute-done.1.got_last
  37.3 2.4 %collective-permute-done.2.got2 = f32[232,128]{1,0:T(8,128)S(1)} collective-permute-done((f32[232,128]{1,0:T(8,128)S(1)}, f32[232,128]{1,0:T(8,128)S(1)}, u32[]{:S(2)}, u32[]{:S(2)}) %collective-permute-start.2) | collective-permute-done | bytes 118816 | tf_op jit(solution)/shard_map/ppermute | solution.py:530
  39.8 0.8 %shard_map.86 = (f32[3,128,128]{2,1,0:T(8,128)S(1)}, f32[4,48,128]{2,1,0:T(8,128)S(1)}) custom-call(f32[3,128,128]{2,1,0:T(8,128)S(1)} %get-tuple-element.38.rim, f32[128,128]{1,0:T(8,128)S(1)} %get-tuple-element.39.rim_diag, f32[8,128]{1,0:T(8,128)S(1)} %get-tuple-element.40.corner_diag, f32[232,128]{1,0:T(8,128)S(1)} %collective-permute-done.got_first, ...), custom_call_target="tpu_custom_call" | custom-call | flops 1000000 | bytes 1000000 | tf_op jit(solution)/shard_map/pallas_call | solution.py:533
  40.6 8.2 %all_to_all.11.got = f32[4,48,128]{2,1,0:T(8,128)S(1)} all-to-all(f32[4,48,128]{2,1,0:T(8,128)S(1)} %get-tuple-element.52), channel_id=1, replica_groups=mesh['curve'=256,'group'=4] {'group'}, dimensions={0} | all-to-all | bytes 196608 | tf_op jit(solution)/shard_map/all_to_all | solution.py:536
  48.8 1.2 %shard_map.87 = f32[3,512,128]{2,1,0:T(8,128)} custom-call(f32[3,512,128]{2,1,0:T(8,128)S(1)} %get-tuple-element.36.early_state, f32[3,512,128]{2,1,0:T(8,128)S(1)} %get-tuple-element.37.late_state, f32[3,128,128]{2,1,0:T(8,128)S(1)} %get-tuple-element.51.fix, f32[4,48,128]{2,1,0:T(8,128)S(1)} %all_to_all.11.got, f32[24,128]{1,0:T(8,128)S(1)} %get-tuple-element.32.codes), custom_call_target="tpu_custom_call" | custom-call | flops 1000000 | bytes 1000000 | tf_op jit(solution)/shard_map/pallas_call | solution.py:537
  (1 shorter events, 0.0 us)
Async XLA Ops:
  0.0 14.5 %copy-start.1 = (f32[4,128,128]{2,1,0:T(8,128)S(1)}, f32[4,128,128]{2,1,0:T(8,128)}, u32[]{:S(2)}) copy-start(f32[4,128,128]{2,1,0:T(8,128)} %interp.5) | copy-start | bytes 786436
  1.5 13.0 %copy-start = (f32[3,16,32,128]{3,2,1,0:T(8,128)S(1)}, f32[3,16,32,128]{3,2,1,0:T(8,128)}, u32[]{:S(2)}) copy-start(f32[3,16,32,128]{3,2,1,0:T(8,128)} %source.1) | copy-start | bytes 2359300
  15.6 21.8 %collective-permute-start = (f32[232,128]{1,0:T(8,128)S(1)}, f32[232,128]{1,0:T(8,128)S(1)}, u32[]{:S(2)}, u32[]{:S(2)}) collective-permute-start(f32[232,128]{1,0:T(8,128)S(1)} %get-tuple-element.41), channel_id=1, source_target_pairs={{256,260},{260,256},{512,516},{516,512},{768,772},{772,768},{257,2... | collective-permute-start | bytes 356360 | tf_op jit(solution)/shard_map/ppermute | solution.py:529
  17.5 19.8 %collective-permute-start.1 = (f32[232,128]{1,0:T(8,128)S(1)}, f32[232,128]{1,0:T(8,128)S(1)}, u32[]{:S(2)}, u32[]{:S(2)}) collective-permute-start(f32[232,128]{1,0:T(8,128)S(1)} %get-tuple-element.41), channel_id=1, source_target_pairs={{0,4},{4,0},{8,12},{12,8},{16,20},{20,16},{24,28},{28,24},{32,36},... | collective-permute-start | bytes 356360 | tf_op jit(solution)/shard_map/ppermute | solution.py:531
  20.3 19.4 %collective-permute-start.2 = (f32[232,128]{1,0:T(8,128)S(1)}, f32[232,128]{1,0:T(8,128)S(1)}, u32[]{:S(2)}, u32[]{:S(2)}) collective-permute-start(f32[232,128]{1,0:T(8,128)S(1)} %get-tuple-element.42), channel_id=1, source_target_pairs={{4,8},{12,16},{20,24},{28,32},{36,40},{44,48},{52,56},{60,64},{68,... | collective-permute-start | bytes 356360 | tf_op jit(solution)/shard_map/ppermute | solution.py:530

commit v5 on v4

--- a/solution.py
+++ b/solution.py
@@ -75,20 +75,22 @@
     copies = [
         pltpu.make_async_copy(parents, p_scalar, sems.at[0]),
         pltpu.make_async_copy(counts, c_scalar, sems.at[1]),
-        pltpu.make_async_copy(field.at[0], f_all.at[0], sems.at[2]),
-        pltpu.make_async_copy(field.at[1], f_all.at[1], sems.at[3]),
-        pltpu.make_async_copy(field.at[2], f_all.at[2], sems.at[4]),
-        pltpu.make_async_copy(children, child, sems.at[5]),
-        pltpu.make_async_copy(kinds, kind, sems.at[6]),
-        pltpu.make_async_copy(parents, p_lane, sems.at[7]),
-        pltpu.make_async_copy(source.at[:, :, 0, :], s_edge.at[0], sems.at[8]),
-        pltpu.make_async_copy(source.at[:, :, 31, :], s_edge.at[1], sems.at[9]),
-        pltpu.make_async_copy(mass, m_all, sems.at[10]),
+        pltpu.make_async_copy(children, child, sems.at[2]),
+        pltpu.make_async_copy(kinds, kind, sems.at[3]),
+        pltpu.make_async_copy(parents, p_lane, sems.at[4]),
+    ]
+    for part in range(12):
+        at = (part // 4, slice(part % 4 * 128, part % 4 * 128 + 128))
+        copies.append(pltpu.make_async_copy(field.at[at], f_all.at[at], sems.at[5 + part]))
+    copies = copies + [
+        pltpu.make_async_copy(source.at[:, :, 0, :], s_edge.at[0], sems.at[17]),
+        pltpu.make_async_copy(source.at[:, :, 31, :], s_edge.at[1], sems.at[18]),
+        pltpu.make_async_copy(mass, m_all, sems.at[19]),
     ]
     for copy in copies:
         copy.start()
     g = lax.axis_index("group")
-    for copy in (copies[0], copies[1], *copies[5:8]):
+    for copy in copies[:5]:
         copy.wait()
     target = filled_group(c_scalar)
     slots = lax.broadcasted_iota(jnp.int32, (1, 16), 1)
@@ -99,7 +101,7 @@
     for at in (0, 8):
         codes[at : at + 1, :] = lane_codes(codes.at[at : at + 8, :])
     codes[16:24, :] = jnp.full((8, 128), target.astype(F32))
-    for copy in copies[2:5]:
+    for copy in copies[5:17]:
         copy.wait()
     for d in range(5):
         for k in range(8):
@@ -117,7 +119,7 @@
                 near = 3 if d == 4 else d - p + 1
                 if 0 <= near < 4 and (d == 4 or near < 3):
                     out[p, c * PICK + near * 8 : c * PICK + near * 8 + 8, :] = part
-    for copy in copies[8:]:
+    for copy in copies[17:]:
         copy.wait()
     block = child[0, 0]
     y = block & 31
@@ -170,7 +172,8 @@
     for pair in range(2):
         wanted = (place + (half + 2 * pair) * 512).astype(F32)
         picked.append(jnp.where(codes == wanted, 1.0, 0.0).T)
-    return jnp.concatenate(picked, axis=0).astype(BF16)
+    picked = jnp.concatenate(picked, axis=0).astype(BF16)
+    return jnp.concatenate([picked, picked], axis=1)
 
 
 def slot_rows(got, near, target, d):
@@ -183,20 +186,16 @@
     return jnp.concatenate(rows, axis=0)
 
 
-def contributions(rows, table_h, table_l):
+def times(rows, table_h, table_l):
     high, low = split(rows)
-    product = dot(high, table_h) + dot(low, table_h) + dot(high, table_l)
-    return split(
-        jnp.concatenate(
-            [
-                jnp.concatenate(
-                    [product[64 * c : 64 * c + 64, 128 * k : 128 * k + 128] for c in range(3)], axis=1
-                )
-                for k in range(4)
-            ],
-            axis=0,
-        )
-    )
+    return dot(high, table_h) + dot(low, table_h) + dot(high, table_l)
+
+
+def arranged(product):
+    blocks = [
+        [product[64 * c : 64 * c + 64, 128 * k : 128 * k + 128] for c in range(3)] for k in range(4)
+    ]
+    return split(jnp.concatenate([jnp.concatenate(b, axis=1) for b in blocks], axis=0))
 
 
 def stacked(interp):
@@ -217,28 +216,33 @@
     target = codes[16:24, :]
     table_h, table_l = stacked(interp)
     own = codes[8:9, :]
-    high, low = contributions(slot_rows(got, 1, target, g), table_h, table_l)
+    line = lax.broadcasted_iota(jnp.int32, (8, 128), 0)
+    wanted = ((line >> 1) * 32 + (line & 1) * 15).astype(F32)
+    parts = [slot_rows(got, 1, target, g)]
+    for side in range(2):
+        _, s = neighbour(g, side)
+        theirs = lane_codes(got.at[s, A_CODE : A_CODE + 8, :])
+        chosen = jnp.where(theirs == wanted, 1.0, 0.0).astype(BF16)
+        rows = slot_rows(got, 2 * side, target, s)
+        both = split(jnp.concatenate([rows[64 * c : 64 * c + 64] for c in range(3)], axis=1))
+        merged = dot(chosen, jnp.concatenate(both, axis=0))
+        parts += [merged[:, 128 * c : 128 * c + 128] for c in range(3)]
+    product = times(jnp.concatenate(parts, axis=0), table_h, table_l)
+    high, low = arranged(product[0:192])
     y_high[...] = high
     y_low[...] = low
+    chosen = jnp.concatenate([selection(own, 0, 64, 512), selection(own, 448, 64, 512)], axis=0)
+    added = dot(chosen, high) + dot(chosen, low)
     for end, start in ((0, 0), (64, 448)):
-        chosen = selection(own, start, 64, 512)
-        added = dot(chosen, high) + dot(chosen, low)
         rim_diag[end : end + 64, :] = OMEGA / (6.0 + mass[start : start + 64, :])
         for c in range(3):
-            rim[c, end : end + 64, :] = field[c, start : start + 64, :] + added[:, c * 128 : c * 128 + 128]
+            more = added[end : end + 64, c * 128 : c * 128 + 128]
+            rim[c, end : end + 64, :] = field[c, start : start + 64, :] + more
 
     corner_diag[...] = jnp.zeros((8, 128), F32)
-    line = lax.broadcasted_iota(jnp.int32, (8, 64), 0)
-    wanted = ((line >> 1) * 32 + (line & 1) * 15).astype(F32)
+    corners[...] = jnp.zeros((2, 8, 128), F32)
     for side in range(2):
         exists, s = neighbour(g, side)
-        theirs = lane_codes(got.at[s, A_CODE : A_CODE + 8, :])
-        chosen = jnp.where(theirs[:, 0:64] == wanted, 1.0, 0.0).astype(BF16)
-        rows = slot_rows(got, 2 * side, target, s)
-        high, low = split(jnp.concatenate([rows[64 * c : 64 * c + 64] for c in range(3)], axis=1))
-        merged = dot(chosen, high) + dot(chosen, low)
-        high, low = split(jnp.concatenate([merged[:, 128 * c : 128 * c + 128] for c in range(3)], axis=0))
-        product = dot(high, table_h) + dot(low, table_h) + dot(high, table_l)
         for end in range(2):
             x = 15 * end
             at = 2 * side + end
@@ -246,7 +250,7 @@
             for c in range(3):
                 value = got[s, A_EDGE + 16 * c + x : A_EDGE + 16 * c + x + 1, :]
                 for k in range(4):
-                    line_at = 8 * c + 2 * k + end
+                    line_at = 192 + 24 * side + 8 * c + 2 * k + end
                     value = value + product[line_at : line_at + 1, 128 * k : 128 * k + 128]
                 corners[end, 4 * side + c : 4 * side + c + 1, :] = jnp.where(exists, value, 0.0)
 
@@ -296,8 +300,9 @@
             copy.start()
         g = lax.axis_index("group")
         target = codes[16:24, :]
-        for k in range(4):
-            table_h[k], table_l[k] = split(interp[k])
+        stack_h, stack_l = stacked(interp)
+        table_h[...] = stack_h
+        table_l[...] = stack_l
         own = codes[8:9, :]
         sel[...] = edge_selection(own)
         for q in range(4):
@@ -308,10 +313,9 @@
             for c in range(3):
                 cst[c, rows, :] = field[c, rows, :] + added[:, c * 128 : c * 128 + 128]
 
-        stack_h, stack_l = stacked(interp)
         for side in range(2):
             exists, s = neighbour(g, side)
-            high, low = contributions(slot_rows(got, 2 * side, target, s), stack_h, stack_l)
+            high, low = arranged(times(slot_rows(got, 2 * side, target, s), stack_h, stack_l))
             chosen = selection(lane_codes(got.at[s, A_CODE : A_CODE + 8, :]), 0, 32, 32)
             added = dot(chosen, high) + dot(chosen, low)
             beyond = got[s, A_DIAG : A_DIAG + 16, :]
@@ -369,17 +373,17 @@
             beside = beyond + row_pair(first, left, right) + z_pair(first)
             fix[c, pl.ds(at, 32), :] = first * THIRD + d_edge * beside
             fix[c, pl.ds(inner, 32), :] = d_inner * first
-    high, low = split(jnp.concatenate([fix[c] for c in range(3)], axis=1))
+    both = jnp.concatenate(split(jnp.concatenate([fix[c] for c in range(3)], axis=1)), axis=0)
 
     def finish(base, sel, table_h, table_l):
-        rows = dot(sel[...], high) + dot(sel[...], low)
-        total = None
+        rows = dot(sel[...], both)
+        placed = []
         for k in range(4):
             at = slice(64 * k, 64 * k + 64)
-            placed = [base[c, at, :] + rows[at, 128 * c : 128 * c + 128] for c in range(3)]
-            p_high, p_low = split(jnp.concatenate(placed, axis=0))
-            product = dot_t(p_high, table_h[k]) + dot_t(p_low, table_h[k]) + dot_t(p_high, table_l[k])
-            total = product if total is None else total + product
+            blocks = [base[c, at, :] + rows[at, 128 * c : 128 * c + 128] for c in range(3)]
+            placed.append(jnp.concatenate(blocks, axis=0))
+        high, low = split(jnp.concatenate(placed, axis=1))
+        total = dot_t(high, table_h[...]) + dot_t(low, table_h[...]) + dot_t(high, table_l[...])
         for s in range(4):
             for c in range(3):
                 out[s, 16 * c : 16 * c + 16, :] = total[64 * c + 16 * s : 64 * c + 16 * s + 16, :]
@@ -404,14 +408,14 @@
         ],
         axis=1,
     )
-    high, low = split(rows)
-    place = lax.broadcasted_iota(jnp.int32, (128, 64), 0)
+    both = jnp.concatenate(split(rows), axis=0)
+    place = lax.broadcasted_iota(jnp.int32, (128, 128), 0)
 
     def finish(state):
         copies = []
         for q in range(4):
-            picked = jnp.where(total[:, 0:64] == (place + q * 128).astype(F32), 1.0, 0.0).astype(BF16)
-            added = dot(picked, high) + dot(picked, low)
+            picked = jnp.where(total == (place + q * 128).astype(F32), 1.0, 0.0).astype(BF16)
+            added = dot(picked, both)
             for c in range(3):
                 at = slice(q * 128, q * 128 + 128)
                 final = state[c, at, :] + added[:, c * 128 : c * 128 + 128]
@@ -473,7 +477,7 @@
             pltpu.VMEM(parents.shape, jnp.int32),
             pltpu.VMEM(parents.shape, jnp.int32),
             pltpu.VMEM((120, 128), F32),
-            pltpu.SemaphoreType.DMA((11,)),
+            pltpu.SemaphoreType.DMA((20,)),
         ],
     )(*map(stay, (field.reshape(3, 512, 128), source, mass.reshape(512, 128), parents, counts, children, kinds)))
     source = source.reshape(3, 512, 128)
@@ -499,9 +503,9 @@
             [
                 shape(3, 512, 128),
                 shape(3, 256, 128),
-                shape(256, 128, kind=BF16),
-                shape(4, 128, 128, kind=BF16),
-                shape(4, 128, 128, kind=BF16),
+                shape(256, 256, kind=BF16),
+                shape(128, 512, kind=BF16),
+                shape(128, 512, kind=BF16),
                 *(shape(*p.shape) for p in pay),
             ],
             [VMEM] * 8 + [HBM] * 2 + [VMEM] * len(pay),

time: 50.2 us -> 50.2 us (level)
  no operation moved by 1% of the time
where the time goes in v5:
time: 50.2 us; the launch traced here: 49.9 us
  blocking collectives  21.2 us (42%)
  starting transfers between devices  19.5 us (39%)
  Pallas kernels  6.69 us (13%)
  waiting for transfers between devices  2.44 us (5%)
    all_to_all x2, blocking collectives, local(): got = lax.all_to_all(send, 'group', 0, 0, tiled=True)  21.2 us
    ppermute x1, starting transfers between devices, local(): got2 = lax.ppermute(pay2, 'curve', outer)  16.9 us
    ppermute x1, waiting for transfers between devices, local(): got2 = lax.ppermute(pay2, 'curve', outer)  2.43 us
    pallas_call x2, Pallas kernels, smoothed(): call(functools.partial(smooth, early), [shape(3, 512, 128), shape(3, 256,...  2.19 us
    ppermute x1, starting transfers between devices, local(): got_first = lax.ppermute(pay1, 'curve', inner_first)  1.92 us
    pallas_call x1, Pallas kernels, local(): call(pack, [shape(4, A_ROWS, 128), shape(24, 128), shape(3, 512, 128), sh...  1.68 us
    pallas_call x1, Pallas kernels, local(): call(collect, shape(3, 512, 128), [VMEM] * 5, [pltpu.VMEM((3, 512, 128),...  1.16 us
  transfers between devices with their start and end apart: 3, of which 1 were waited for; matrix products, arithmetic and copies ran while one was open for 0% of the time, Pallas kernels for 4%

profile of v5, /device:TPU:6, one launch (start us, length us, event | category | flops | bytes accessed | tf_op | source)
XLA Modules:
  0.0 49.9 jit_solution(10509100126456105295)
XLA Ops:
  0.0 0.0 copy-start.1
  0.0 1.7 %shard_map.82 = (f32[4,216,128]{2,1,0:T(8,128)S(1)}, f32[24,128]{1,0:T(8,128)S(1)}, f32[3,512,128]{2,1,0:T(8,128)S(1)}, f32[512,128]{1,0:T(8,128)S(1)}) custom-call(f32[3,512,128]{2,1,0:T(8,128)} %bitcast.7, f32[3,16,32,128]{3,2,1,0:T(8,128)} %source.1, f32[512,128]{1,0:T(8,128)} %bitcast.8, s32[1,1,4,16]{3,2,1,0:T(4,128)} %parents.1, s32[1,1,4]{2,1,0:T(1,128)} %counts.1, ...), custom_call_target="tpu_custom_call" | custom-call | flops 1000000 | bytes 1000000 | tf_op jit(solution)/shard_map/pallas_call | solution.py:468
  1.7 0.0 copy-start
  1.7 13.0 %all_to_all.10.got = f32[4,216,128]{2,1,0:T(8,128)S(1)} all-to-all(f32[4,216,128]{2,1,0:T(8,128)S(1)} %get-tuple-element.29), channel_id=1, replica_groups=mesh['curve'=256,'group'=4] {'group'}, dimensions={0} | all-to-all | bytes 884736 | tf_op jit(solution)/shard_map/all_to_all | solution.py:484
  14.7 0.0 copy-done.1
  14.7 0.0 copy-done
  14.7 0.9 %shard_map.83 = (f32[232,128]{1,0:T(8,128)S(1)}, f32[232,128]{1,0:T(8,128)S(1)}, f32[3,128,128]{2,1,0:T(8,128)S(1)}, f32[128,128]{1,0:T(8,128)S(1)}, f32[8,128]{...) custom-call(f32[4,216,128]{2,1,0:T(8,128)S(1)} %all_to_all.10.got, ...), custom_call_target="tpu_custom_call" | custom-call | flops 1000000 | bytes 1000000 | tf_op jit(solution)/shard_map/pallas_call | solution.py:485
  15.6 1.9 %collective-permute-start = (f32[232,128]{1,0:T(8,128)S(1)}, f32[232,128]{1,0:T(8,128)S(1)}, u32[]{:S(2)}, u32[]{:S(2)}) collective-permute-start(f32[232,128]{1,0:T(8,128)S(1)} %get-tuple-element.41), channel_id=1, source_target_pairs={{256,260},{260,256},{512,516},{516,512},{768,772},{772,768},{257,2... | collective-permute-start | bytes 356360 | tf_op jit(solution)/shard_map/ppermute | solution.py:533
  17.6 0.7 %collective-permute-start.1 = (f32[232,128]{1,0:T(8,128)S(1)}, f32[232,128]{1,0:T(8,128)S(1)}, u32[]{:S(2)}, u32[]{:S(2)}) collective-permute-start(f32[232,128]{1,0:T(8,128)S(1)} %get-tuple-element.41), channel_id=1, source_target_pairs={{0,4},{4,0},{8,12},{12,8},{16,20},{20,16},{24,28},{28,24},{32,36},... | collective-permute-start | bytes 356360 | tf_op jit(solution)/shard_map/ppermute | solution.py:535
  18.2 2.2 %shard_map.84 = (f32[3,512,128]{2,1,0:T(8,128)S(1)}, f32[3,256,128]{2,1,0:T(8,128)S(1)}, bf16[256,256]{1,0:T(8,128)(2,1)S(1)}, bf16[128,512]{1,0:T(8,128)(2,1)S(...) custom-call(f32[4,216,128]{2,1,0:T(8,128)S(1)} %all_to_all.10.got, f32[3,512,128]{2,1,0:T(8,128)S(1)} %get-tuple-element.30.field, ...), custom_call_target="tpu_custom_call" | custom-call | flops 20000000 | bytes 8000000 | tf_op jit(solution)/shard_map/pallas_call | solution.py:501
  20.4 16.9 %collective-permute-start.2 = (f32[232,128]{1,0:T(8,128)S(1)}, f32[232,128]{1,0:T(8,128)S(1)}, u32[]{:S(2)}, u32[]{:S(2)}) collective-permute-start(f32[232,128]{1,0:T(8,128)S(1)} %get-tuple-element.42), channel_id=1, source_target_pairs={{4,8},{12,16},{20,24},{28,32},{36,40},{44,48},{52,56},{60,64},{68,... | collective-permute-start | bytes 356360 | tf_op jit(solution)/shard_map/ppermute | solution.py:534
  37.4 0.0 collective-permute-done.got_first
  37.4 0.0 collective-permute-done.1.got_last
  37.4 2.4 %collective-permute-done.2.got2 = f32[232,128]{1,0:T(8,128)S(1)} collective-permute-done((f32[232,128]{1,0:T(8,128)S(1)}, f32[232,128]{1,0:T(8,128)S(1)}, u32[]{:S(2)}, u32[]{:S(2)}) %collective-permute-start.2) | collective-permute-done | bytes 118816 | tf_op jit(solution)/shard_map/ppermute | solution.py:534
  39.9 0.7 %shard_map.86 = (f32[3,128,128]{2,1,0:T(8,128)S(1)}, f32[4,48,128]{2,1,0:T(8,128)S(1)}) custom-call(f32[3,128,128]{2,1,0:T(8,128)S(1)} %get-tuple-element.38.rim, f32[128,128]{1,0:T(8,128)S(1)} %get-tuple-element.39.rim_diag, f32[8,128]{1,0:T(8,128)S(1)} %get-tuple-element.40.corner_diag, f32[232,128]{1,0:T(8,128)S(1)} %collective-permute-done.got_first, ...), custom_call_target="tpu_custom_call" | custom-call | flops 1000000 | bytes 1000000 | tf_op jit(solution)/shard_map/pallas_call | solution.py:537
  40.6 8.2 %all_to_all.11.got = f32[4,48,128]{2,1,0:T(8,128)S(1)} all-to-all(f32[4,48,128]{2,1,0:T(8,128)S(1)} %get-tuple-element.52), channel_id=1, replica_groups=mesh['curve'=256,'group'=4] {'group'}, dimensions={0} | all-to-all | bytes 196608 | tf_op jit(solution)/shard_map/all_to_all | solution.py:540
  48.8 1.2 %shard_map.87 = f32[3,512,128]{2,1,0:T(8,128)} custom-call(f32[3,512,128]{2,1,0:T(8,128)S(1)} %get-tuple-element.36.early_state, f32[3,512,128]{2,1,0:T(8,128)S(1)} %get-tuple-element.37.late_state, f32[3,128,128]{2,1,0:T(8,128)S(1)} %get-tuple-element.51.fix, f32[4,48,128]{2,1,0:T(8,128)S(1)} %all_to_all.11.got, f32[24,128]{1,0:T(8,128)S(1)} %get-tuple-element.32.codes), custom_call_target="tpu_custom_call" | custom-call | flops 1000000 | bytes 1000000 | tf_op jit(solution)/shard_map/pallas_call | solution.py:541
  (1 shorter events, 0.0 us)
Async XLA Ops:
  0.0 14.7 %copy-start.1 = (f32[4,128,128]{2,1,0:T(8,128)S(1)}, f32[4,128,128]{2,1,0:T(8,128)}, u32[]{:S(2)}) copy-start(f32[4,128,128]{2,1,0:T(8,128)} %interp.5) | copy-start | bytes 786436
  1.7 13.0 %copy-start = (f32[3,16,32,128]{3,2,1,0:T(8,128)S(1)}, f32[3,16,32,128]{3,2,1,0:T(8,128)}, u32[]{:S(2)}) copy-start(f32[3,16,32,128]{3,2,1,0:T(8,128)} %source.1) | copy-start | bytes 2359300
  15.6 21.8 %collective-permute-start = (f32[232,128]{1,0:T(8,128)S(1)}, f32[232,128]{1,0:T(8,128)S(1)}, u32[]{:S(2)}, u32[]{:S(2)}) collective-permute-start(f32[232,128]{1,0:T(8,128)S(1)} %get-tuple-element.41), channel_id=1, source_target_pairs={{256,260},{260,256},{512,516},{516,512},{768,772},{772,768},{257,2... | collective-permute-start | bytes 356360 | tf_op jit(solution)/shard_map/ppermute | solution.py:533
  17.6 19.8 %collective-permute-start.1 = (f32[232,128]{1,0:T(8,128)S(1)}, f32[232,128]{1,0:T(8,128)S(1)}, u32[]{:S(2)}, u32[]{:S(2)}) collective-permute-start(f32[232,128]{1,0:T(8,128)S(1)} %get-tuple-element.41), channel_id=1, source_target_pairs={{0,4},{4,0},{8,12},{12,8},{16,20},{20,16},{24,28},{28,24},{32,36},... | collective-permute-start | bytes 356360 | tf_op jit(solution)/shard_map/ppermute | solution.py:535
  20.4 19.5 %collective-permute-start.2 = (f32[232,128]{1,0:T(8,128)S(1)}, f32[232,128]{1,0:T(8,128)S(1)}, u32[]{:S(2)}, u32[]{:S(2)}) collective-permute-start(f32[232,128]{1,0:T(8,128)S(1)} %get-tuple-element.42), channel_id=1, source_target_pairs={{4,8},{12,16},{20,24},{28,32},{36,40},{44,48},{52,56},{60,64},{68,... | collective-permute-start | bytes 356360 | tf_op jit(solution)/shard_map/ppermute | solution.py:534

commit v6 on v5

--- a/solution.py
+++ b/solution.py
@@ -79,13 +79,12 @@
         pltpu.make_async_copy(kinds, kind, sems.at[3]),
         pltpu.make_async_copy(parents, p_lane, sems.at[4]),
     ]
-    for part in range(12):
-        at = (part // 4, slice(part % 4 * 128, part % 4 * 128 + 128))
-        copies.append(pltpu.make_async_copy(field.at[at], f_all.at[at], sems.at[5 + part]))
+    for c in range(3):
+        copies.append(pltpu.make_async_copy(field.at[c], f_all.at[c], sems.at[5 + c]))
     copies = copies + [
-        pltpu.make_async_copy(source.at[:, :, 0, :], s_edge.at[0], sems.at[17]),
-        pltpu.make_async_copy(source.at[:, :, 31, :], s_edge.at[1], sems.at[18]),
-        pltpu.make_async_copy(mass, m_all, sems.at[19]),
+        pltpu.make_async_copy(source.at[:, :, 0, :], s_edge.at[0], sems.at[8]),
+        pltpu.make_async_copy(source.at[:, :, 31, :], s_edge.at[1], sems.at[9]),
+        pltpu.make_async_copy(mass, m_all, sems.at[10]),
     ]
     for copy in copies:
         copy.start()
@@ -101,12 +100,11 @@
     for at in (0, 8):
         codes[at : at + 1, :] = lane_codes(codes.at[at : at + 8, :])
     codes[16:24, :] = jnp.full((8, 128), target.astype(F32))
-    for copy in copies[5:17]:
-        copy.wait()
-    for d in range(5):
-        for k in range(8):
-            p = p_scalar[0, 0, d, k] if d < 4 else p_scalar[0, 0, target, 8 + k]
-            for c in range(3):
+    for c in range(3):
+        copies[5 + c].wait()
+        for d in range(5):
+            for k in range(8):
+                p = p_scalar[0, 0, d, k] if d < 4 else p_scalar[0, 0, target, 8 + k]
                 j = c * 40 + d * 8 + k
                 rows[j : j + 1, :] = f_all[c, pl.ds(p, 1), :]
     slot = lax.broadcasted_iota(jnp.int32, (8, 128), 0)
@@ -119,7 +117,7 @@
                 near = 3 if d == 4 else d - p + 1
                 if 0 <= near < 4 and (d == 4 or near < 3):
                     out[p, c * PICK + near * 8 : c * PICK + near * 8 + 8, :] = part
-    for copy in copies[17:]:
+    for copy in copies[8:]:
         copy.wait()
     block = child[0, 0]
     y = block & 31
@@ -355,11 +353,12 @@
                     base[c, pl.ds(row, 1), :] = state[c, pl.ds(b, 1), :] - cst[c, pl.ds(b, 1), :]
 
 
-def restrict(rim, rim_diag, corner_diag, got_first, got_last, got2, *rest):
+def restrict(rim, rim_diag, corner_diag, got_first, got_last, got_out, got_back, *rest):
     early_set, late_set, (fix, out) = rest[:4], rest[4:8], rest[8:]
     odd = lax.axis_index("curve") & 1
     got1 = jnp.where(waits(), got_first[...], got_last[...])
-    for got, upper in ((got1, 1 - odd), (got2[...], odd)):
+    got2 = jnp.where(odd == 1, got_back[...], got_out[...])
+    for got, upper in ((got1, 1 - odd), (got2, odd)):
         at = pl.multiple_of(upper * 96, 32)
         inner = pl.multiple_of(upper * 32 + 32, 32)
         d_edge = rim_diag[pl.ds(at, 32), :]
@@ -477,7 +476,7 @@
             pltpu.VMEM(parents.shape, jnp.int32),
             pltpu.VMEM(parents.shape, jnp.int32),
             pltpu.VMEM((120, 128), F32),
-            pltpu.SemaphoreType.DMA((20,)),
+            pltpu.SemaphoreType.DMA((11,)),
         ],
     )(*map(stay, (field.reshape(3, 512, 128), source, mass.reshape(512, 128), parents, counts, children, kinds)))
     source = source.reshape(3, 512, 128)
@@ -523,20 +522,20 @@
             moved=8_000_000,
         )(got, field, source, mass, interp, y_high, y_low, codes, stay(children), stay(kinds), *pay)
 
-    *early_set, pay2 = smoothed(True, pay2)
+    *early_set, back = smoothed(True, pay2)
     count = lax.axis_size("curve")
     waiting = [i for i in range(64, count) if i % 64 < 2]
     inner_first = [(i, i ^ 1) for i in waiting]
     inner_last = [(i, i ^ 1) for i in range(count) if i not in waiting]
-    outer = [(i, i + 1) for i in range(1, count - 1, 2)]
-    outer = outer + [(b, a) for a, b in outer]
+    outward = [(i, i + 1) for i in range(1, count - 1, 2)]
+    got_out = lax.ppermute(pay2, "curve", outward)
     got_first = lax.ppermute(pay1, "curve", inner_first)
-    got2 = lax.ppermute(pay2, "curve", outer)
+    got_back = lax.ppermute(back, "curve", [(b, a) for a, b in outward])
     got_last = lax.ppermute(pay1, "curve", inner_last)
     late_set = smoothed(False)
     fix, send = call(
-        restrict, [shape(3, 128, 128), shape(4, 48, 128)], [VMEM] * 14
-    )(rim, rim_diag, corner_diag, got_first, got_last, got2, *early_set[1:], *late_set[1:])
+        restrict, [shape(3, 128, 128), shape(4, 48, 128)], [VMEM] * 15
+    )(rim, rim_diag, corner_diag, got_first, got_last, got_out, got_back, *early_set[1:], *late_set[1:])
     got = lax.all_to_all(send, "group", 0, 0, tiled=True)
     out = call(
         collect,

time: 50.2 us -> 53.7 us (1.070)
  waiting for transfers between devices: 2.44 us -> 6.89 us
  starting transfers between devices: 19.5 us -> 18.7 us
    ppermute x1 -> x2, waiting for transfers between devices: 2.43 us -> 6.89 us  [the longest x1 6.88 us: local(): got_out = lax.ppermute(pay2, 'curve', outward)]
    ppermute x1 -> x2, starting transfers between devices: 16.9 us -> 16.1 us  [the longest x1 14.8 us: local(): got_back = lax.ppermute(back, 'curve', [(b, a) for a, b in outward])]
  transfers between devices with their start and end apart: 3 -> 4, of which waited for: 1 -> 1; matrix products, arithmetic and copies ran while one was open for 0% -> 0% of each run, Pallas kernels for 4% -> 0%
where the time goes in v6:
time: 53.7 us; the launch traced here: 53.4 us
  blocking collectives  21.2 us (39%)
  starting transfers between devices  18.7 us (35%)
  waiting for transfers between devices  6.89 us (13%)
  Pallas kernels  6.53 us (12%)
    all_to_all x2, blocking collectives, local(): got = lax.all_to_all(send, 'group', 0, 0, tiled=True)  21.2 us
    ppermute x1, starting transfers between devices, local(): got_back = lax.ppermute(back, 'curve', [(b, a) for a, b in outward])  14.8 us
    ppermute x1, waiting for transfers between devices, local(): got_out = lax.ppermute(pay2, 'curve', outward)  6.88 us
    pallas_call x2, Pallas kernels, smoothed(): call(functools.partial(smooth, early), [shape(3, 512, 128), shape(3, 256,...  2.2 us
    ppermute x1, starting transfers between devices, local(): got_first = lax.ppermute(pay1, 'curve', inner_first)  1.92 us
    pallas_call x1, Pallas kernels, local(): call(pack, [shape(4, A_ROWS, 128), shape(24, 128), shape(3, 512, 128), sh...  1.52 us
    ppermute x1, starting transfers between devices, local(): got_out = lax.ppermute(pay2, 'curve', outward)  1.29 us
    pallas_call x1, Pallas kernels, local(): call(collect, shape(3, 512, 128), [VMEM] * 5, [pltpu.VMEM((3, 512, 128),...  1.16 us
  transfers between devices with their start and end apart: 4, of which 1 were waited for; matrix products, arithmetic and copies ran while one was open for 0% of the time, Pallas kernels for 0%

profile of v6, /device:TPU:6, one launch (start us, length us, event | category | flops | bytes accessed | tf_op | source)
XLA Modules:
  0.0 53.4 jit_solution(11631431259806028221)
XLA Ops:
  0.0 0.0 copy-start.1
  0.0 1.5 %shard_map.82 = (f32[4,216,128]{2,1,0:T(8,128)S(1)}, f32[24,128]{1,0:T(8,128)S(1)}, f32[3,512,128]{2,1,0:T(8,128)S(1)}, f32[512,128]{1,0:T(8,128)S(1)}) custom-call(f32[3,512,128]{2,1,0:T(8,128)} %bitcast.7, f32[3,16,32,128]{3,2,1,0:T(8,128)} %source.1, f32[512,128]{1,0:T(8,128)} %bitcast.8, s32[1,1,4,16]{3,2,1,0:T(4,128)} %parents.1, s32[1,1,4]{2,1,0:T(1,128)} %counts.1, ...), custom_call_target="tpu_custom_call" | custom-call | flops 1000000 | bytes 1000000 | tf_op jit(solution)/shard_map/pallas_call | solution.py:467
  1.5 0.0 copy-start
  1.5 13.0 %all_to_all.10.got = f32[4,216,128]{2,1,0:T(8,128)S(1)} all-to-all(f32[4,216,128]{2,1,0:T(8,128)S(1)} %get-tuple-element.29), channel_id=1, replica_groups=mesh['curve'=256,'group'=4] {'group'}, dimensions={0} | all-to-all | bytes 884736 | tf_op jit(solution)/shard_map/all_to_all | solution.py:483
  14.5 0.0 copy-done.1
  14.5 0.0 copy-done
  14.5 0.9 %shard_map.83 = (f32[232,128]{1,0:T(8,128)S(1)}, f32[232,128]{1,0:T(8,128)S(1)}, f32[3,128,128]{2,1,0:T(8,128)S(1)}, f32[128,128]{1,0:T(8,128)S(1)}, f32[8,128]{...) custom-call(f32[4,216,128]{2,1,0:T(8,128)S(1)} %all_to_all.10.got, ...), custom_call_target="tpu_custom_call" | custom-call | flops 1000000 | bytes 1000000 | tf_op jit(solution)/shard_map/pallas_call | solution.py:484
  15.5 2.2 %shard_map.84 = (f32[3,512,128]{2,1,0:T(8,128)S(1)}, f32[3,256,128]{2,1,0:T(8,128)S(1)}, bf16[256,256]{1,0:T(8,128)(2,1)S(1)}, bf16[128,512]{1,0:T(8,128)(2,1)S(...) custom-call(f32[4,216,128]{2,1,0:T(8,128)S(1)} %all_to_all.10.got, f32[3,512,128]{2,1,0:T(8,128)S(1)} %get-tuple-element.30.field, ...), custom_call_target="tpu_custom_call" | custom-call | flops 20000000 | bytes 8000000 | tf_op jit(solution)/shard_map/pallas_call | solution.py:500
  17.6 14.8 %collective-permute-start.3 = (f32[232,128]{1,0:T(8,128)S(1)}, f32[232,128]{1,0:T(8,128)S(1)}, u32[]{:S(2)}, u32[]{:S(2)}) collective-permute-start(f32[232,128]{1,0:T(8,128)S(1)} %get-tuple-element.42), channel_id=1, source_target_pairs={{8,4},{16,12},{24,20},{32,28},{40,36},{48,44},{56,52},{64,60},{72,... | collective-permute-start | bytes 356360 | tf_op jit(solution)/shard_map/ppermute | solution.py:533
  32.5 1.9 %collective-permute-start = (f32[232,128]{1,0:T(8,128)S(1)}, f32[232,128]{1,0:T(8,128)S(1)}, u32[]{:S(2)}, u32[]{:S(2)}) collective-permute-start(f32[232,128]{1,0:T(8,128)S(1)} %get-tuple-element.41), channel_id=1, source_target_pairs={{256,260},{260,256},{512,516},{516,512},{768,772},{772,768},{257,2... | collective-permute-start | bytes 356360 | tf_op jit(solution)/shard_map/ppermute | solution.py:532
  34.4 0.7 %collective-permute-start.1 = (f32[232,128]{1,0:T(8,128)S(1)}, f32[232,128]{1,0:T(8,128)S(1)}, u32[]{:S(2)}, u32[]{:S(2)}) collective-permute-start(f32[232,128]{1,0:T(8,128)S(1)} %get-tuple-element.41), channel_id=1, source_target_pairs={{0,4},{4,0},{8,12},{12,8},{16,20},{20,16},{24,28},{28,24},{32,36},... | collective-permute-start | bytes 356360 | tf_op jit(solution)/shard_map/ppermute | solution.py:534
  35.1 1.3 %collective-permute-start.2 = (f32[232,128]{1,0:T(8,128)S(1)}, f32[232,128]{1,0:T(8,128)S(1)}, u32[]{:S(2)}, u32[]{:S(2)}) collective-permute-start(f32[232,128]{1,0:T(8,128)S(1)} %get-tuple-element.35.rest_0_), channel_id=1, source_target_pairs={{4,8},{12,16},{20,24},{28,32},{36,40},{44,48},{52,56},{60,64},{68,... | collective-permute-start | bytes 356360 | tf_op jit(solution)/shard_map/ppermute | solution.py:531
  36.4 0.0 collective-permute-done.3.got_back
  36.4 0.0 collective-permute-done.got_first
  36.5 0.0 collective-permute-done.1.got_last
  36.5 6.9 %collective-permute-done.2.got_out = f32[232,128]{1,0:T(8,128)S(1)} collective-permute-done((f32[232,128]{1,0:T(8,128)S(1)}, f32[232,128]{1,0:T(8,128)S(1)}, u32[]{:S(2)}, u32[]{:S(2)}) %collective-permute-start.2) | collective-permute-done | bytes 118816 | tf_op jit(solution)/shard_map/ppermute | solution.py:531
  43.3 0.7 %shard_map.86 = (f32[3,128,128]{2,1,0:T(8,128)S(1)}, f32[4,48,128]{2,1,0:T(8,128)S(1)}) custom-call(f32[3,128,128]{2,1,0:T(8,128)S(1)} %get-tuple-element.38.rim, f32[128,128]{1,0:T(8,128)S(1)} %get-tuple-element.39.rim_diag, f32[8,128]{1,0:T(8,128)S(1)} %get-tuple-element.40.corner_diag, f32[232,128]{1,0:T(8,128)S(1)} %collective-permute-done.got_first, ...), custom_call_target="tpu_custom_call" | custom-call | flops 1000000 | bytes 1000000 | tf_op jit(solution)/shard_map/pallas_call | solution.py:536
  44.1 8.2 %all_to_all.11.got = f32[4,48,128]{2,1,0:T(8,128)S(1)} all-to-all(f32[4,48,128]{2,1,0:T(8,128)S(1)} %get-tuple-element.52), channel_id=1, replica_groups=mesh['curve'=256,'group'=4] {'group'}, dimensions={0} | all-to-all | bytes 196608 | tf_op jit(solution)/shard_map/all_to_all | solution.py:539
  52.3 1.2 %shard_map.87 = f32[3,512,128]{2,1,0:T(8,128)} custom-call(f32[3,512,128]{2,1,0:T(8,128)S(1)} %get-tuple-element.36.early_state, f32[3,512,128]{2,1,0:T(8,128)S(1)} %get-tuple-element.37.late_state, f32[3,128,128]{2,1,0:T(8,128)S(1)} %get-tuple-element.51.fix, f32[4,48,128]{2,1,0:T(8,128)S(1)} %all_to_all.11.got, f32[24,128]{1,0:T(8,128)S(1)} %get-tuple-element.32.codes), custom_call_target="tpu_custom_call" | custom-call | flops 1000000 | bytes 1000000 | tf_op jit(solution)/shard_map/pallas_call | solution.py:540
  (1 shorter events, 0.0 us)
Async XLA Ops:
  0.0 14.5 %copy-start.1 = (f32[4,128,128]{2,1,0:T(8,128)S(1)}, f32[4,128,128]{2,1,0:T(8,128)}, u32[]{:S(2)}) copy-start(f32[4,128,128]{2,1,0:T(8,128)} %interp.5) | copy-start | bytes 786436
  1.5 13.0 %copy-start = (f32[3,16,32,128]{3,2,1,0:T(8,128)S(1)}, f32[3,16,32,128]{3,2,1,0:T(8,128)}, u32[]{:S(2)}) copy-start(f32[3,16,32,128]{3,2,1,0:T(8,128)} %source.1) | copy-start | bytes 2359300
  17.6 18.8 %collective-permute-start.3 = (f32[232,128]{1,0:T(8,128)S(1)}, f32[232,128]{1,0:T(8,128)S(1)}, u32[]{:S(2)}, u32[]{:S(2)}) collective-permute-start(f32[232,128]{1,0:T(8,128)S(1)} %get-tuple-element.42), channel_id=1, source_target_pairs={{8,4},{16,12},{24,20},{32,28},{40,36},{48,44},{56,52},{64,60},{72,... | collective-permute-start | bytes 356360 | tf_op jit(solution)/shard_map/ppermute | solution.py:533
  32.5 4.0 %collective-permute-start = (f32[232,128]{1,0:T(8,128)S(1)}, f32[232,128]{1,0:T(8,128)S(1)}, u32[]{:S(2)}, u32[]{:S(2)}) collective-permute-start(f32[232,128]{1,0:T(8,128)S(1)} %get-tuple-element.41), channel_id=1, source_target_pairs={{256,260},{260,256},{512,516},{516,512},{768,772},{772,768},{257,2... | collective-permute-start | bytes 356360 | tf_op jit(solution)/shard_map/ppermute | solution.py:532
  34.4 2.1 %collective-permute-start.1 = (f32[232,128]{1,0:T(8,128)S(1)}, f32[232,128]{1,0:T(8,128)S(1)}, u32[]{:S(2)}, u32[]{:S(2)}) collective-permute-start(f32[232,128]{1,0:T(8,128)S(1)} %get-tuple-element.41), channel_id=1, source_target_pairs={{0,4},{4,0},{8,12},{12,8},{16,20},{20,16},{24,28},{28,24},{32,36},... | collective-permute-start | bytes 356360 | tf_op jit(solution)/shard_map/ppermute | solution.py:534
  35.1 8.3 %collective-permute-start.2 = (f32[232,128]{1,0:T(8,128)S(1)}, f32[232,128]{1,0:T(8,128)S(1)}, u32[]{:S(2)}, u32[]{:S(2)}) collective-permute-start(f32[232,128]{1,0:T(8,128)S(1)} %get-tuple-element.35.rest_0_), channel_id=1, source_target_pairs={{4,8},{12,16},{20,24},{28,32},{36,40},{44,48},{52,56},{60,64},{68,... | collective-permute-start | bytes 356360 | tf_op jit(solution)/shard_map/ppermute | solution.py:531
